TPU v7x, 128 devices: a whole 4x4x4 slice. The times are simulated.
128 devices in a mesh: lat: 32 (over z, x, core), lev: 4 (over y).
Axes of the slice: x: 4, y: 4, z: 4, core: 2. Of those that a mesh axis runs over, the one named last changes fastest.
Arguments:
- fields: float32 [3, 16, 1024, 4096], P(None, 'lev', 'lat'), may hold values from -6 to 6
- velocity: float32 [2, 16, 1024, 4096], P(None, 'lev', 'lat'), may hold values from -6 to 6
- surface: float32 [1024, 4096], P('lat'), may hold values from -6 to 6
- thickness: float32 [16], P('lev'), may hold values from 0.02 to 0.2
- row_owner: int32 [1024], P('lat'), may hold values from -1 to 31, as said below
Outputs:
- new_fields: float32 [3, 16, 1024, 4096], P(None, 'lev', 'lat')
- geopotential: float32 [16, 1024, 4096], P('lev', 'lat')
- polar_rows: float32 [3, 16, 512, 4096], P(None, 'lev', 'lat')
Inputs may be any that keep to these rules, and one draw needn't show every extreme that they name: `row_owner`: exactly the rows j < 256 and j >= 768 hold a device index, all others -1. Of the rows held by one device p, exactly 16 name p and the other 16 name the device (p + 32 / 2) mod 32.
All inputs are finite; a program needn't handle non-finite values.
Results may differ from a plain program's by a relative error of at most 0.0003.
Values sent between devices are 32-bit elements; how exact they have to be, the bound alone decides.
A program may use at most 128 MiB of HBM per device.

v0:
```python
import math

import jax
import jax.numpy as jnp
from jax import lax
from jax.sharding import PartitionSpec as P

PASSES = 8


courant_lon = 0.3
courant_lat = 0.3
diffuse_lon = 0.04
diffuse_lat = 0.08
base_temp = 3.0


def shifted(array, axis, by):
    size = lax.axis_size(axis)
    return lax.ppermute(array, axis, [(i, (i + by) % size) for i in range(size)])


def with_halo(cells, sides, width):
    for axis, dim in sides:
        count = lax.axis_size(axis)
        ends = count - 1
        head = lax.slice_in_dim(cells, 0, width, axis=dim)
        tail = lax.slice_in_dim(cells, cells.shape[dim] - width, cells.shape[dim], axis=dim)
        cells = jnp.concatenate(
            [
                lax.ppermute(tail, axis, [(i, (i + 1) % count) for i in range(ends)]),
                cells,
                lax.ppermute(head, axis, [((i + 1) % count, i) for i in range(ends)]),
            ],
            axis=dim,
        )
    return cells


def laid_out(blocks, dim):
    blocks = jnp.moveaxis(blocks, 0, dim)
    lengths = blocks.shape
    return blocks.reshape(*lengths[:dim], lengths[dim] * lengths[dim + 1], *lengths[dim + 2 :])


def copy_for_each(array, axis):
    size = lax.axis_size(axis)
    return lax.all_to_all(
        jnp.broadcast_to(array[None], (size, *array.shape)), axis, 0, 0, tiled=True
    )


def gather_directly(array, axis, dim):
    return laid_out(copy_for_each(array, axis), dim)


def row_tables(start, row_count, all_rows):
    row_index = start + jnp.arange(row_count)
    row_ids = row_index.astype(jnp.float32)
    spacing = math.pi / all_rows
    lat_mid = -0.5 * math.pi + (row_ids + 0.5) * spacing
    cos_mid = jnp.cos(lat_mid)
    metric = 1.0 / jnp.maximum(cos_mid, 0.25)
    cos_north = jnp.cos(lat_mid + 0.5 * spacing)
    cos_south = jnp.cos(lat_mid - 0.5 * spacing)
    polar = (row_index < all_rows // 4) | (row_index >= all_rows - all_rows // 4)
    strength = jnp.where(polar, 0.05 + 0.2 * (1.0 - cos_mid / math.cos(0.25 * math.pi)), 0.0)
    return (metric[:, None], cos_north[:, None], cos_south[:, None], strength[:, None])


def strength_at(positions, all_rows):
    spacing = math.pi / all_rows
    lat_mid = -0.5 * math.pi + (positions + 0.5) * spacing
    cos_mid = jnp.cos(lat_mid)
    polar = (positions < all_rows // 4) | (positions >= all_rows - all_rows // 4)
    return jnp.where(polar, 0.05 + 0.2 * (1.0 - cos_mid / math.cos(0.25 * math.pi)), 0.0)


def advect(state, wind_u, wind_v, north_rows, south_rows, metric, cos_north, cos_south):
    east_cell = jnp.roll(state, -1, axis=-1)
    west_cell = jnp.roll(state, 1, axis=-1)
    result = state - courant_lon * metric * wind_u * (east_cell - west_cell) * 0.5
    result = result - courant_lat * wind_v * (north_rows - south_rows) * 0.5
    result = result + diffuse_lon * metric * metric * (east_cell - 2.0 * state + west_cell)
    return result + diffuse_lat * metric * (
        cos_north * (north_rows - state) - cos_south * (state - south_rows)
    )


def minmod(left_val, right_val):
    return (
        0.5
        * (jnp.sign(left_val) + jnp.sign(right_val))
        * jnp.minimum(jnp.abs(left_val), jnp.abs(right_val))
    )


def smooth(state, strength):
    for pass_index in range(PASSES):
        slopes = jnp.roll(state, -1, axis=-1) - state
        limited = minmod(
            slopes, minmod(jnp.roll(slopes, 1, axis=-1), jnp.roll(slopes, -1, axis=-1))
        )
        fluxes = strength * (slopes - limited)
        state = state + fluxes - jnp.roll(fluxes, 1, axis=-1)
    return state


def take_rows(source_data, source_rows, live_rows):
    return jnp.where(live_rows[:, None], jnp.take(source_data, source_rows, axis=2), 0.0)


def slot_rows(selected, local_rows, half_rows):
    earlier = local_rows[None, :] < local_rows[:, None]
    rank = jnp.sum((selected[None, :] & earlier).astype(jnp.int32), axis=1)
    rank_slots = jnp.arange(half_rows)[:, None]
    picked = selected[None, :] & (rank[None, :] == rank_slots)
    source = jnp.sum(picked.astype(jnp.int32) * local_rows[None, :], axis=1)
    return (source, jnp.any(picked, axis=1))


def trip_compact(payload, half_axis):
    return shifted((payload[0], payload[1]), "lat", half_axis)


def local(fields, velocity, surface, thickness, row_owner):
    lat_count = lax.axis_size("lat")
    own_index = lax.axis_index("lat")
    row_count = fields.shape[2]
    all_rows = row_count * lat_count
    quarter = lat_count // 4
    half_rows = row_count // 2
    half_axis = lat_count // 2
    metric, cos_north, cos_south, strength = row_tables(own_index * row_count, row_count, all_rows)
    padded = with_halo(fields, (("lat", 2),), 1)
    below_row = jnp.where(own_index == 0, fields[:, :, :1], padded[:, :, :1])
    above_row = jnp.where(own_index == lat_count - 1, fields[:, :, -1:], padded[:, :, -1:])
    north_rows = jnp.concatenate([padded[:, :, 2:-1], above_row], axis=2)
    south_rows = jnp.concatenate([below_row, padded[:, :, 1:-2]], axis=2)
    advected = advect(
        fields, velocity[0], velocity[1], north_rows, south_rows, metric, cos_north, cos_south
    )
    weight = (base_temp + advected[0]) * thickness[:, None, None]
    column = jnp.sum(weight, axis=0)
    gathered = gather_directly(column[None], "lev", 0)
    level_ids = jnp.arange(gathered.shape[0])
    outside = jnp.sum(
        jnp.where((level_ids > lax.axis_index("lev"))[:, None, None], gathered, 0.0), axis=0
    )
    geopotential = (
        surface[None] + outside[None] + (column[None] - jnp.cumsum(weight, axis=0)) + 0.5 * weight
    )
    local_rows = jnp.arange(row_count)
    row_pos = (own_index * row_count + local_rows).astype(jnp.float32)
    same_owner = row_owner[:, None] == row_owner[None, :]
    earlier = local_rows[None, :] < local_rows[:, None]
    row_rank = jnp.sum((same_owner & earlier).astype(jnp.int32), axis=1)
    kept_rows = row_owner == own_index
    remote = (row_owner >= 0) & (row_owner != own_index)
    keep_from, keep_live = slot_rows(kept_rows, local_rows, half_rows)
    polar_device = (own_index < quarter) | (own_index >= lat_count - quarter)
    own_work = take_rows(advected, keep_from, keep_live)
    own_pos = jnp.take(row_pos, keep_from)
    send_from, send_live = slot_rows(remote, local_rows, half_rows)
    out_rows = take_rows(advected, send_from, send_live)
    out_pos = jnp.where(send_live, jnp.take(row_pos, send_from), -1.0)
    got_rows, got_pos = trip_compact((out_rows, out_pos), half_axis)
    work_rows = jnp.where(polar_device, own_work, got_rows)
    work_pos = jnp.where(polar_device, own_pos, got_pos)
    work_strength = strength_at(work_pos, all_rows)[:, None]
    polar_rows = smooth(work_rows, work_strength)
    returning = jnp.where(polar_device, 0.0, polar_rows)
    return_pos = jnp.where(polar_device, -1.0, work_pos)
    back_rows, back_pos = trip_compact((returning, return_pos), half_axis)
    matched = back_pos[None, :] == row_pos[:, None]
    slot_from = jnp.sum(jnp.where(matched, jnp.arange(half_rows)[None, :], 0), axis=1)
    from_back = remote & jnp.any(matched, axis=1)
    kept_slot = jnp.where(kept_rows, row_rank, 0)
    placed = jnp.where(from_back[:, None], jnp.take(back_rows, slot_from, axis=2), advected)
    new_fields = jnp.where(kept_rows[:, None], jnp.take(polar_rows, kept_slot, axis=2), placed)
    return (new_fields, geopotential, polar_rows)


def solution(mesh):
    in_specs = (
        P(None, "lev", "lat", None),
        P(None, "lev", "lat", None),
        P("lat", None),
        P("lev"),
        P("lat"),
    )
    out_specs = (P(None, "lev", "lat", None), P("lev", "lat", None), P(None, "lev", "lat", None))
    return jax.shard_map(local, mesh=mesh, in_specs=in_specs, out_specs=out_specs, check_vma=False)
```

profile of v0, /device:TPU:38, one launch (start us, length us, event | category | flops | bytes accessed | tf_op | source)
XLA Modules:
  0.0 428.3 jit_solution(7052032487194017120)
XLA Ops:
  0.6 6.8 %copy.55 = f32[3,4,32,4096]{3,1,2,0:T(4,128)S(1)} copy(f32[3,4,32,4096]{3,2,1,0:T(8,128)} %param.11) | data formatting | bytes 12582912 | tf_op args[0]
  7.5 2.7 copy-done
  12.4 2.7 collective-permute-start.1
  15.1 13.9 %fusion.17 = (f32[3,4,31,4096]{3,1,2,0:T(4,128)}, f32[3,4,31,4096]{3,1,2,0:T(4,128)}) fusion(f32[3,4,32,4096]{3,1,2,0:T(4,128)} %copy-done), kind=kLoop, calls=%fused_computation.117 | loop fusion | bytes 24379392 | tf_op jit(solution)/shard_map/slice | solution.py:138
  29.0 12.6 %fusion.15 = (f32[3,4,32,4095]{3,1,2,0:T(4,128)}, f32[3,4,32,4095]{3,1,2,0:T(4,128)}) fusion(f32[3,4,32,4096]{3,1,2,0:T(4,128)} %copy-done), kind=kLoop, calls=%fused_computation.115 | loop fusion | bytes 25159680 | tf_op jit(solution)/shard_map/jit(_roll_static)/slice | solution.py:80
  44.0 2.7 multiply_bitcast_fusion.1
  48.1 2.7 copy.50
  52.7 20.1 %multiply_add_fusion = f32[3,4,32,4096]{3,1,2,0:T(4,128)} fusion(f32[3,4,31,4096]{3,1,2,0:T(4,128)} %get-tuple-element.31, f32[3,4,1,4096]{3,1,2,0:T(4,128)S(1)} %get-tuple-element.33, f32[3,4,1,4096]{3,1,2,0:T(4,128)S(1)} %get-tuple-element.32, f32[3,4,31,4096]{3,1,2,0:T(4,128)} %get-tuple-element.30, f32[3,4,32,4095]{3,1,2,0:T(4,128)} %get-tuple-element.27, ...), kind=kLoop, calls=%fused_computation.14 | loop fusion | flops 37748736 | bytes 41943552 | tf_op jit(solution)/shard_map/add | solution.py:85
  72.8 5.2 %gather_fusion.1 = f32[16,3,4,4096]{3,2,1,0:T(4,128)S(1)} fusion(f32[3,4,32,4096]{3,1,2,0:T(4,128)} %multiply_add_fusion, s32[1024]{0:T(1024)S(1)} %pad_clamp_fusion.2), kind=kCustom, calls=%fused_computation.3.clone | custom fusion | bytes 6291520 | tf_op jit(solution)/shard_map/jit(_take)/gather | solution.py:110
  78.0 2.8 bitcast_select_fusion.1
  80.8 3.0 collective-permute-start.2
  85.6 66.5 %collective-permute-done.3 = f32[16]{0:T(128)S(1)} collective-permute-done((f32[16]{0:T(128)S(1)}, f32[16]{0:T(128)S(1)}, u32[]{:S(2)}, u32[]{:S(2)}) %collective-permute-start.3) | collective-permute-done | bytes 96 | tf_op jit(solution)/shard_map/ppermute | solution.py:20
  152.2 5.2 %gather_fusion = f32[16,3,4,4096]{3,2,1,0:T(4,128)S(1)} fusion(f32[3,4,32,4096]{3,1,2,0:T(4,128)} %multiply_add_fusion, s32[1024]{0:T(1024)S(1)} %pad_clamp_fusion.3), kind=kCustom, calls=%fused_computation.clone | custom fusion | bytes 6291520 | tf_op jit(solution)/shard_map/jit(_take)/gather | solution.py:110
  157.4 3.6 fusion.1
  166.5 10.2 %subtract_multiply_fusion.7 = f32[3,4,16,4096]{3,1,0,2:T(4,128)S(1)} fusion(f32[3,4,16,4096]{3,1,0,2:T(4,128)S(1)} %maximum_subtract_fusion, f32[3,4,16,1]{3,1,0,2:T(4,128)S(1)} %get-tuple-element.67, f32[3,4,16,4095]{3,1,0,2:T(4,128)S(1)} %get-tuple-element.69, f32[3,4,16,4095]{3,1,0,2:T(4,128)S(1)} %get-tuple-element.68, ...), kind=kLoop, calls=%fused_computation.57 | loop fusion | flops 15728640 | bytes 12582976 | tf_op jit(solution)/shard_map/mul | solution.py:104
  184.8 10.4 %subtract_multiply_fusion.6 = f32[3,4,16,4096]{3,1,0,2:T(4,128)S(1)} fusion(f32[3,4,16,4096]{3,1,0,2:T(4,128)S(1)} %maximum_subtract_fusion.2, f32[3,4,16,1]{3,1,0,2:T(4,128)S(1)} %get-tuple-element.63, f32[3,4,16,4095]{3,1,0,2:T(4,128)S(1)} %get-tuple-element.65, f32[3,4,16,4095]{3,1,0,2:T(4,128)S(1)} %get-tuple-element.64, ...), kind=kLoop, calls=%fused_computation.56 | loop fusion | flops 15728640 | bytes 12582976 | tf_op jit(solution)/shard_map/mul | solution.py:104
  203.4 10.2 %subtract_multiply_fusion.5 = f32[3,4,16,4096]{3,1,0,2:T(4,128)S(1)} fusion(f32[3,4,16,4096]{3,1,0,2:T(4,128)S(1)} %maximum_subtract_fusion.4, f32[3,4,16,1]{3,1,0,2:T(4,128)S(1)} %get-tuple-element.59, f32[3,4,16,4095]{3,1,0,2:T(4,128)S(1)} %get-tuple-element.61, f32[3,4,16,4095]{3,1,0,2:T(4,128)S(1)} %get-tuple-element.60, ...), kind=kLoop, calls=%fused_computation.55 | loop fusion | flops 15728640 | bytes 12582976 | tf_op jit(solution)/shard_map/mul | solution.py:104
  221.6 10.6 %subtract_multiply_fusion.4 = f32[3,4,16,4096]{3,1,0,2:T(4,128)S(1)} fusion(f32[3,4,16,4096]{3,1,0,2:T(4,128)S(1)} %maximum_subtract_fusion.6, f32[3,4,16,1]{3,1,0,2:T(4,128)S(1)} %get-tuple-element.55, f32[3,4,16,4095]{3,1,0,2:T(4,128)S(1)} %get-tuple-element.57, f32[3,4,16,4095]{3,1,0,2:T(4,128)S(1)} %get-tuple-element.56, ...), kind=kLoop, calls=%fused_computation.54 | loop fusion | flops 15728640 | bytes 12582976 | tf_op jit(solution)/shard_map/mul | solution.py:104
  240.3 10.1 %subtract_multiply_fusion.3 = f32[3,4,16,4096]{3,1,0,2:T(4,128)S(1)} fusion(f32[3,4,16,4096]{3,1,0,2:T(4,128)S(1)} %maximum_subtract_fusion.8, f32[3,4,16,1]{3,1,0,2:T(4,128)S(1)} %get-tuple-element.51, f32[3,4,16,4095]{3,1,0,2:T(4,128)S(1)} %get-tuple-element.53, f32[3,4,16,4095]{3,1,0,2:T(4,128)S(1)} %get-tuple-element.52, ...), kind=kLoop, calls=%fused_computation.53 | loop fusion | flops 15728640 | bytes 12582976 | tf_op jit(solution)/shard_map/mul | solution.py:104
  258.5 10.3 %subtract_multiply_fusion.2 = f32[3,4,16,4096]{3,1,0,2:T(4,128)S(1)} fusion(f32[3,4,16,4096]{3,1,0,2:T(4,128)S(1)} %maximum_subtract_fusion.10, f32[3,4,16,1]{3,1,0,2:T(4,128)S(1)} %get-tuple-element.47, f32[3,4,16,4095]{3,1,0,2:T(4,128)S(1)} %get-tuple-element.49, f32[3,4,16,4095]{3,1,0,2:T(4,128)S(1)} %get-tuple-element.48, ...), kind=kLoop, calls=%fused_computation.52 | loop fusion | flops 15728640 | bytes 12582976 | tf_op jit(solution)/shard_map/mul | solution.py:104
  276.8 10.4 %subtract_multiply_fusion.1 = f32[3,4,16,4096]{3,1,0,2:T(4,128)S(1)} fusion(f32[3,4,16,4096]{3,1,0,2:T(4,128)S(1)} %maximum_subtract_fusion.12, f32[3,4,16,1]{3,1,0,2:T(4,128)S(1)} %get-tuple-element.43, f32[3,4,16,4095]{3,1,0,2:T(4,128)S(1)} %get-tuple-element.45, f32[3,4,16,4095]{3,1,0,2:T(4,128)S(1)} %get-tuple-element.44, ...), kind=kLoop, calls=%fused_computation.51 | loop fusion | flops 15728640 | bytes 12582976 | tf_op jit(solution)/shard_map/mul | solution.py:104
  295.4 9.9 %subtract_multiply_fusion = f32[3,4,16,4096]{3,1,0,2:T(4,128)S(1)} fusion(f32[3,4,16,4096]{3,1,0,2:T(4,128)S(1)} %maximum_subtract_fusion.14, f32[3,4,16,1]{3,1,0,2:T(4,128)S(1)} %get-tuple-element.39, f32[3,4,16,4095]{3,1,0,2:T(4,128)S(1)} %get-tuple-element.41, f32[3,4,16,4095]{3,1,0,2:T(4,128)S(1)} %get-tuple-element.40, ...), kind=kLoop, calls=%fused_computation.50 | loop fusion | flops 15728640 | bytes 12582976 | tf_op jit(solution)/shard_map/mul | solution.py:104
  305.5 3.7 broadcast_select_fusion
  311.3 3.4 fusion.13
  316.3 4.5 %all-to-all-start = ((f32[4,1,32,4096]{3,2,1,0:T(8,128)}), f32[4,1,32,4096]{3,2,1,0:T(8,128)}, u32[]{:S(2)}, u32[]{:S(2)}) async-start(f32[4,1,32,4096]{3,2,1,0:T(8,128)} %broadcast_in_dim.140), calls=%async_computation | async-start | bytes 4194304 | tf_op jit(solution)/shard_map/all_to_all | solution.py:48
  322.3 59.4 %collective-permute-done.4 = f32[16]{0:T(128)S(1)} collective-permute-done((f32[16]{0:T(128)S(1)}, f32[16]{0:T(128)S(1)}, u32[]{:S(2)}, u32[]{:S(2)}) %collective-permute-start.4) | collective-permute-done | bytes 96 | tf_op jit(solution)/shard_map/ppermute | solution.py:20
  381.9 5.0 %reduce_window_sum.11 = f32[4,32,4096]{2,0,1:T(4,128)} reduce-window(f32[4,32,4096]{2,0,1:T(4,128)S(1)} %get-tuple-element.16, f32[]{:T(128)} %constant.28.clone.1), window={size=4x1x1 pad=3_0x0_0x0_0}, to_apply=%region_11.15 | reduce-window | flops 1572864 | bytes 4194308 | tf_op jit(solution)/shard_map/jit(cumsum)/reduce_window_sum | solution.py:151
  393.2 3.5 copy.70
  396.7 6.6 %gather_fusion.4 = f32[32,3,4,4096]{3,2,1,0:T(4,128)} fusion(f32[3,4,16,4096]{3,1,2,0:T(4,128)S(1)} %copy.64, s32[1024]{0:T(1024)S(1)} %pad_clamp_fusion.1), kind=kCustom, calls=%fused_computation.2.clone | custom fusion | bytes 12583040 | tf_op jit(solution)/shard_map/jit(_take)/gather | solution.py:180
  405.4 6.9 %gather_fusion.5 = f32[32,3,4,4096]{3,2,1,0:T(4,128)} fusion(f32[3,4,16,4096]{3,1,2,0:T(4,128)S(1)} %copy.66, s32[1024]{0:T(1024)S(1)} %pad_clamp_fusion), kind=kCustom, calls=%fused_computation.5.clone | custom fusion | bytes 12583040 | tf_op jit(solution)/shard_map/jit(_take)/gather | solution.py:179
  412.2 9.2 %fusion = f32[3,4,32,4096]{3,1,2,0:T(4,128)S(1)} fusion(f32[3,4,32,4096]{3,1,2,0:T(4,128)} %multiply_add_fusion, f32[32,3,4,4096]{3,2,1,0:T(4,128)} %gather_fusion.5, f32[32,3,4,4096]{3,2,1,0:T(4,128)} %gather_fusion.4, pred[32]{0:T(512)(128)(4,1)S(1)} %compare_and_fusion, pred[32]{0:T(512)(128)(4,1)S(1)} %copy-done.4, pred[32]{0:T(512)(128)(4,1)S(1)} %and.65, ...), kind=kLoop, calls=%fused_computation.11 | loop fusion | flops 6291456 | bytes 25165952 | tf_op jit(solution)/shard_map/jit(_where)/select_n | solution.py:180
  421.5 6.3 %copy.68 = f32[3,4,32,4096]{3,2,1,0:T(8,128)} copy(f32[3,4,32,4096]{3,1,2,0:T(4,128)S(1)} %fusion) | data formatting | bytes 12582912
  (123 shorter events, 85.4 us)
Async XLA Ops:
  7.5 2.7 copy-start
  10.2 41.2 %collective-permute-start = (f32[3,4,1,4096]{3,1,2,0:T(4,128)S(1)}, f32[3,4,1,4096]{3,1,2,0:T(4,128)S(1)}, u32[]{:S(2)}, u32[]{:S(2)}) collective-permute-start(f32[3,4,1,4096]{3,1,2,0:T(4,128)S(1)} %get-tuple-element.34), channel_id=1, source_target_pairs={{4,0},{8,4},{12,8},{16,12},{20,16},{24,20},{28,24},{32,28},{36,32}... | collective-permute-start | bytes 589832 | tf_op jit(solution)/shard_map/ppermute | solution.py:33
  12.4 39.1 %collective-permute-start.1 = (f32[3,4,1,4096]{3,1,2,0:T(4,128)S(1)}, f32[3,4,1,4096]{3,1,2,0:T(4,128)S(1)}, u32[]{:S(2)}, u32[]{:S(2)}) collective-permute-start(f32[3,4,1,4096]{3,1,2,0:T(4,128)S(1)} %get-tuple-element.35), channel_id=1, source_target_pairs={{0,4},{4,8},{8,12},{12,16},{16,20},{20,24},{24,28},{28,32},{32,36}... | collective-permute-start | bytes 589832 | tf_op jit(solution)/shard_map/ppermute | solution.py:31
  29.0 14.0 %copy-start.7 = (s32[32]{0:T(128)S(1)}, s32[32]{0:T(128)}, u32[]{:S(2)}) copy-start(s32[32]{0:T(128)} %param.15) | copy-start | bytes 388
  43.7 3.0 copy-start.8
  80.8 76.6 %collective-permute-start.2 = (f32[3,4,16,4096]{3,1,0,2:T(4,128)}, f32[3,4,16,4096]{3,1,0,2:T(4,128)}, u32[]{:S(2)}, u32[]{:S(2)}) collective-permute-start(f32[3,4,16,4096]{3,1,0,2:T(4,128)} %bitcast_select_fusion.1), channel_id=1, source_target_pairs={{0,64},{4,68},{8,72},{12,76},{16,80},{20,84},{24,88},{28,92},{32,9... | collective-permute-start | bytes 9437192 | tf_op jit(solution)/shard_map/ppermute | solution.py:20
  83.8 68.3 %collective-permute-start.3 = (f32[16]{0:T(128)S(1)}, f32[16]{0:T(128)S(1)}, u32[]{:S(2)}, u32[]{:S(2)}) collective-permute-start(f32[16]{0:T(128)S(1)} %get-tuple-element.24), channel_id=1, source_target_pairs={{0,64},{4,68},{8,72},{12,76},{16,80},{20,84},{24,88},{28,92},{32,9... | collective-permute-start | bytes 200 | tf_op jit(solution)/shard_map/ppermute | solution.py:20
  305.5 5.8 %copy-start.6 = (f32[4]{0:T(128)S(1)}, f32[4]{0:T(128)}, u32[]{:S(2)}) copy-start(f32[4]{0:T(128)} %param.14) | copy-start | bytes 52
  309.2 94.0 %collective-permute-start.5 = (f32[3,4,16,4096]{3,1,0,2:T(4,128)}, f32[3,4,16,4096]{3,1,0,2:T(4,128)}, u32[]{:S(2)}, u32[]{:S(2)}) collective-permute-start(f32[3,4,16,4096]{3,1,0,2:T(4,128)} %get-tuple-element.22), channel_id=1, source_target_pairs={{0,64},{4,68},{8,72},{12,76},{16,80},{20,84},{24,88},{28,92},{32,9... | collective-permute-start | bytes 9437192 | tf_op jit(solution)/shard_map/ppermute | solution.py:20
  314.7 6.0 %copy-start.5 = (s32[32]{0:T(128)S(1)}, s32[32]{0:T(128)}, u32[]{:S(2)}) copy-start(s32[32]{0:T(128)} %get-tuple-element.18) | copy-start | bytes 388
  314.8 67.0 %copy-start.9 = (pred[32]{0:T(512)(128)(4,1)S(1)}, pred[32]{0:T(512)(128)(4,1)}, u32[]{:S(2)}) copy-start(pred[32]{0:T(512)(128)(4,1)} %copy-done.8) | copy-start | bytes 100
  316.3 70.7 %all-to-all-start = ((f32[4,1,32,4096]{3,2,1,0:T(8,128)}), f32[4,1,32,4096]{3,2,1,0:T(8,128)}, u32[]{:S(2)}, u32[]{:S(2)}) async-start(f32[4,1,32,4096]{3,2,1,0:T(8,128)} %broadcast_in_dim.140), calls=%async_computation | async-start | bytes 4194304 | tf_op jit(solution)/shard_map/all_to_all | solution.py:48
  320.8 60.9 %collective-permute-start.4 = (f32[16]{0:T(128)S(1)}, f32[16]{0:T(128)S(1)}, u32[]{:S(2)}, u32[]{:S(2)}) collective-permute-start(f32[16]{0:T(128)S(1)} %get-tuple-element.20), channel_id=1, source_target_pairs={{0,64},{4,68},{8,72},{12,76},{16,80},{20,84},{24,88},{28,92},{32,9... | collective-permute-start | bytes 200 | tf_op jit(solution)/shard_map/ppermute | solution.py:20
  381.9 7.1 %copy-start.3 = (f32[32,4096]{1,0:T(8,128)S(1)}, f32[32,4096]{1,0:T(8,128)}, u32[]{:S(2)}) copy-start(f32[32,4096]{1,0:T(8,128)} %param.13) | copy-start | bytes 1572868
  387.0 2.2 copy-start.2
  390.4 2.6 copy-start.1
  405.4 6.9 %copy-start.4 = (pred[32]{0:T(512)(128)(4,1)S(1)}, pred[32]{0:T(512)(128)(4,1)}, u32[]{:S(2)}) copy-start(pred[32]{0:T(512)(128)(4,1)} %get-tuple-element.17) | copy-start | bytes 100
where the time goes:
time: 434 us; the launch traced here: 428 us
  other arithmetic  170 us (39%)
  waiting for transfers between devices  126 us (29%)
  local copies, waits for them, and re-layouts  114 us (26%)
  starting transfers between devices  16.6 us (4%)
    ppermute x4, waiting for transfers between devices, shifted(): lax.ppermute(array, axis, [(i, (i + by) % size) for i in range(size)])  126 us
    mul x8, other arithmetic, smooth(): fluxes = strength * (slopes - limited)  82.1 us
    unnamed x24, local copies, waits for them, and re-layouts  22 us
    add x1, other arithmetic, advect(): result + diffuse_lat * metric * (cos_north * (north_rows - state) - cos_s...  20.1 us
    sub x7, other arithmetic, smooth(): state = state + fluxes - jnp.roll(fluxes, 1, axis=-1)  18 us
    slice x16, local copies, waits for them, and re-layouts, smooth(): jnp.roll(slopes, 1, axis=-1)  16.9 us
    slice x1, local copies, waits for them, and re-layouts, local(): north_rows = jnp.concatenate([padded[:, :, 2:-1], above_row], axis=2)  13.9 us
    slice x2, local copies, waits for them, and re-layouts, advect(): east_cell = jnp.roll(state, -1, axis=-1)  13.8 us
  transfers between devices with their start and end apart: 7, of which 2 were waited for; matrix products, arithmetic and copies ran while one was open for 16% of the time, Pallas kernels for 0%

commit v1 on v0

v1 whole, which is shorter than its diff:
```python
import math

import jax
import jax.numpy as jnp
from jax import lax
from jax.experimental import pallas as pl
from jax.experimental.pallas import tpu as pltpu
from jax.sharding import PartitionSpec as P

PASSES = 8
MESH = pl.DeviceIdType.MESH
LANES = 128

courant_lon = 0.3
courant_lat = 0.3
diffuse_lon = 0.04
diffuse_lat = 0.08
base_temp = 3.0


def filtered(state, strength):
    width = state.shape[1]
    for _ in range(PASSES):
        slope = pltpu.roll(state, width - 1, 1) - state
        west = pltpu.roll(slope, 1, 1)
        east = pltpu.roll(slope, width - 1, 1)
        least = jnp.minimum(slope, jnp.minimum(west, east))
        most = jnp.maximum(slope, jnp.maximum(west, east))
        flux = strength * (slope - jnp.maximum(least, 0.0) - jnp.minimum(most, 0.0))
        state = state + flux - pltpu.roll(flux, 1, 1)
    return state


def make_kernel(lat_count, lev_count, nf, levels, rows, lons, segs):
    half = rows // 2
    slabs = nf * levels
    groups = rows // 8
    seg = lons // segs
    all_rows = rows * lat_count
    spacing = math.pi / all_rows
    shift = lat_count // 2
    quarter = lat_count // 4

    def kernel(
        fields, velocity, surface, thickness, row_owner,
        new_fields, geo, polar_rows,
        cells, wind, ground, halo, below, columns, packed, tables, owners, thick, slots,
        in_sem, wind_sem, small_sem, halo_send, halo_recv, col_send, col_recv, row_send, row_recv,
    ):
        me = lax.axis_index("lat")
        lev = lax.axis_index("lev")
        polar = (me < quarter) | (me >= lat_count - quarter)
        partner = lax.rem(me + shift, lat_count)

        def slab_of(step):
            return step // levels, levels - 1 - lax.rem(step, levels)

        def cell_copy(step):
            q, k = slab_of(step)
            return pltpu.make_async_copy(fields.at[q, k], cells.at[q, k], in_sem.at[step])

        def wind_copy(k, part):
            return pltpu.make_async_copy(velocity.at[part, k], wind.at[part, k], wind_sem.at[part, k])

        own_copy = pltpu.make_async_copy(row_owner, owners, small_sem.at[0])
        thick_copy = pltpu.make_async_copy(thickness, thick, small_sem.at[1])
        ground_copy = pltpu.make_async_copy(surface, ground, small_sem.at[2])

        barrier = pltpu.get_barrier_semaphore()
        for by in (shift, 1, lat_count - 1):
            pl.semaphore_signal(
                barrier, inc=1, device_id={"lat": lax.rem(me + by, lat_count)}, device_id_type=MESH
            )
        for by in range(1, lev_count):
            pl.semaphore_signal(
                barrier, inc=1, device_id={"lev": lax.rem(lev + by, lev_count)}, device_id_type=MESH
            )

        cell_copy(0).start()
        wind_copy(levels - 1, 0).start()
        wind_copy(levels - 1, 1).start()
        own_copy.start()
        thick_copy.start()
        for step in range(1, levels):
            cell_copy(step).start()
            wind_copy(levels - 1 - step, 0).start()
            wind_copy(levels - 1 - step, 1).start()
        for step in range(levels, slabs):
            cell_copy(step).start()
        ground_copy.start()

        row_index = me * rows + lax.broadcasted_iota(jnp.int32, (rows, LANES), 0)
        row_ids = row_index.astype(jnp.float32)
        lat_mid = -0.5 * math.pi + (row_ids + 0.5) * spacing
        cos_mid = jnp.cos(lat_mid)
        metric = 1.0 / jnp.maximum(cos_mid, 0.25)
        cos_north = jnp.cos(lat_mid + 0.5 * spacing)
        cos_south = jnp.cos(lat_mid - 0.5 * spacing)
        is_polar = (row_index < all_rows // 4) | (row_index >= all_rows - all_rows // 4)
        tables[0] = 0.5 * courant_lon * metric
        tables[1] = diffuse_lon * metric * metric
        tables[2] = diffuse_lat * metric * cos_north
        tables[3] = diffuse_lat * metric * cos_south
        tables[4] = jnp.where(
            is_polar, 0.05 + 0.2 * (1.0 - cos_mid / math.cos(0.25 * math.pi)), 0.0
        )

        own_copy.wait()
        thick_copy.wait()
        sent_from = [jnp.int32(0)] * half
        kept_from = [jnp.int32(0)] * half
        sent = jnp.int32(0)
        for row in range(rows):
            away = (owners[row] != me).astype(jnp.int32)
            kept = row - sent
            for slot in range(max(0, row - half), min(half, row + 1)):
                sent_from[slot] = jnp.where((away == 1) & (sent == slot), row, sent_from[slot])
                kept_from[slot] = jnp.where((away == 0) & (kept == slot), row, kept_from[slot])
            sent = sent + away
        for slot in range(half):
            slots[slot] = sent_from[slot]
            slots[half + slot] = kept_from[slot]

        pl.semaphore_wait(barrier, 3 + lev_count - 1)

        to_north = pltpu.make_async_remote_copy(
            src_ref=fields.at[:, :, rows - 1 : rows, :], dst_ref=halo.at[0],
            send_sem=halo_send.at[0], recv_sem=halo_recv.at[0],
            device_id={"lat": lax.rem(me + 1, lat_count)}, device_id_type=MESH,
        )
        to_south = pltpu.make_async_remote_copy(
            src_ref=fields.at[:, :, 0:1, :], dst_ref=halo.at[1],
            send_sem=halo_send.at[1], recv_sem=halo_recv.at[1],
            device_id={"lat": lax.rem(me + lat_count - 1, lat_count)}, device_id_type=MESH,
        )
        own_south = pltpu.make_async_copy(fields.at[:, :, 0:1, :], halo.at[0], halo_recv.at[0])
        own_north = pltpu.make_async_copy(fields.at[:, :, rows - 1 : rows, :], halo.at[1], halo_recv.at[1])
        first = me == 0
        last = me == lat_count - 1

        @pl.when(jnp.logical_not(last))
        def _():
            to_north.start()

        @pl.when(jnp.logical_not(first))
        def _():
            to_south.start()

        @pl.when(first)
        def _():
            own_south.start()

        @pl.when(last)
        def _():
            own_north.start()

        @pl.when(first)
        def _():
            own_south.wait()

        @pl.when(jnp.logical_not(first))
        def _():
            to_north.wait_recv()

        @pl.when(last)
        def _():
            own_north.wait()

        @pl.when(jnp.logical_not(last))
        def _():
            to_south.wait_recv()

        def row_copy(step, part):
            q, k = slab_of(step)
            cols = pl.ds(pl.multiple_of(part * seg, LANES), seg)
            return pltpu.make_async_remote_copy(
                src_ref=packed.at[q, k, :, cols], dst_ref=polar_rows.at[q, k, :, cols],
                send_sem=row_send.at[step, part], recv_sem=row_recv.at[step, part],
                device_id={"lat": partner}, device_id_type=MESH,
            )

        def col_copy(by):
            return pltpu.make_async_remote_copy(
                src_ref=below, dst_ref=columns.at[by - 1],
                send_sem=col_send.at[by - 1], recv_sem=col_recv.at[by - 1],
                device_id={"lev": lax.rem(lev + lev_count - by, lev_count)}, device_id_type=MESH,
            )

        blocks = lons // LANES
        per = seg // LANES

        def window(ref, lead, row, part):
            def at(block, n):
                return ref[(*lead, pl.ds(row, 8), pl.ds(pl.multiple_of(block * LANES, LANES), n * LANES))]

            return jnp.concatenate(
                [
                    at(lax.rem(part * per + blocks - 1, blocks), 1),
                    at(part * per, per),
                    at(lax.rem((part + 1) * per, blocks), 1),
                ],
                axis=1,
            )

        width = seg + 2 * LANES
        sub = lax.broadcasted_iota(jnp.int32, (8, width), 0)

        def spread(table, row):
            one = tables[table, pl.ds(row, 8), :]
            return jnp.concatenate([one] * (width // LANES), axis=1)

        def halo_window(side, q, k, part):
            def at(block, n):
                return halo[side, q, k, :, pl.ds(pl.multiple_of(block * LANES, LANES), n * LANES)]

            whole = jnp.concatenate(
                [
                    at(lax.rem(part * per + blocks - 1, blocks), 1),
                    at(part * per, per),
                    at(lax.rem((part + 1) * per, blocks), 1),
                ],
                axis=1,
            )
            return jnp.broadcast_to(whole, (8, width))

        def one_window(q, k, part, group):
            row = pl.multiple_of(group * 8, 8)
            cols = pl.ds(pl.multiple_of(part * seg, LANES), seg)
            state = window(cells, (q, k), row, part)
            above = pl.multiple_of(jnp.minimum(group + 1, groups - 1) * 8, 8)
            under = pl.multiple_of(jnp.maximum(group - 1, 0) * 8, 8)
            next_row = jnp.where(
                group == groups - 1,
                halo_window(1, q, k, part),
                pltpu.roll(window(cells, (q, k), above, part), 7, 0),
            )
            prev_row = jnp.where(
                group == 0,
                halo_window(0, q, k, part),
                pltpu.roll(window(cells, (q, k), under, part), 1, 0),
            )
            north = jnp.where(sub == 7, next_row, pltpu.roll(state, 7, 0))
            south = jnp.where(sub == 0, prev_row, pltpu.roll(state, 1, 0))
            wind_u = window(wind, (0, k), row, part)
            wind_v = window(wind, (1, k), row, part)
            east = pltpu.roll(state, width - 1, 1)
            west = pltpu.roll(state, 1, 1)
            result = state - spread(0, row) * wind_u * (east - west)
            result = result - (0.5 * courant_lat) * wind_v * (north - south)
            result = result + spread(1, row) * (east - 2.0 * state + west)
            result = result + spread(2, row) * (north - state) - spread(3, row) * (state - south)

            @pl.when(q == 0)
            def _():
                weight = (base_temp + result[:, LANES : LANES + seg]) * thick[k]
                so_far = jnp.where(k == levels - 1, 0.0, below[pl.ds(row, 8), cols])
                geo[k, pl.ds(row, 8), cols] = so_far + 0.5 * weight
                below[pl.ds(row, 8), cols] = so_far + weight

            @pl.when(jnp.logical_not(polar))
            def _():
                new_fields[q, k, pl.ds(row, 8), cols] = result[:, LANES : LANES + seg]

            @pl.when(polar)
            def _():
                smooth = filtered(result, spread(4, row))
                new_fields[q, k, pl.ds(row, 8), cols] = smooth[:, LANES : LANES + seg]

        def one_step(index, carry):
            step = index // segs
            part = lax.rem(index, segs)
            q, k = slab_of(step)
            cols = pl.ds(pl.multiple_of(part * seg, LANES), seg)

            @pl.when(part == 0)
            def _():
                cell_copy(step).wait()

            @pl.when((part == 0) & (step < levels))
            def _():
                wind_copy(k, 0).wait()
                wind_copy(k, 1).wait()

            def one_group(group, carry):
                one_window(q, k, part, group)
                return carry

            lax.fori_loop(0, groups, one_group, 0)

            @pl.when(polar)
            def _():
                for slot in range(half):
                    packed[q, k, slot : slot + 1, cols] = new_fields[q, k, pl.ds(slots[slot], 1), cols]
                row_copy(step, part).start()
                for slot in range(half):
                    polar_rows[q, k, slot : slot + 1, cols] = new_fields[
                        q, k, pl.ds(slots[half + slot], 1), cols
                    ]

            @pl.when((step == levels - 1) & (part == segs - 1))
            def _():
                for by in range(1, lev_count):
                    @pl.when(lev >= by)
                    def _():
                        col_copy(by).start()

            return carry

        lax.fori_loop(0, slabs * segs, one_step, 0)

        ground_copy.wait()
        for by in range(1, lev_count):
            @pl.when(lev + by < lev_count)
            def _():
                col_copy(by).wait_recv()

        def finish(index, carry):
            row = pl.multiple_of(index * 8, 8)
            outside = ground[pl.ds(row, 8), :]
            for by in range(1, lev_count):
                outside = outside + jnp.where(lev + by < lev_count, columns[by - 1, pl.ds(row, 8), :], 0.0)
            for k in range(levels):
                geo[k, pl.ds(row, 8), :] = geo[k, pl.ds(row, 8), :] + outside
            return carry

        lax.fori_loop(0, groups, finish, 0)

        for by in range(1, lev_count):
            @pl.when(lev >= by)
            def _():
                col_copy(by).wait_send()

        @pl.when(jnp.logical_not(last))
        def _():
            to_north.wait_send()

        @pl.when(jnp.logical_not(first))
        def _():
            to_south.wait_send()

        @pl.when(polar)
        def _():
            def drain(index, carry):
                row_copy(index // segs, lax.rem(index, segs)).wait_send()
                return carry

            lax.fori_loop(0, slabs * segs, drain, 0)

        @pl.when(jnp.logical_not(polar))
        def _():
            def arrive(index, carry):
                row_copy(index // segs, lax.rem(index, segs)).wait_recv()
                return carry

            lax.fori_loop(0, slabs * segs, arrive, 0)

    return kernel


def solution(mesh):
    lat_count, lev_count = mesh.shape["lat"], mesh.shape["lev"]
    segs = 4

    def local(fields, velocity, surface, thickness, row_owner):
        nf, levels, rows, lons = fields.shape
        half = rows // 2
        any_spec = pl.BlockSpec(memory_space=pl.ANY)
        vmem_spec = pl.BlockSpec(memory_space=pltpu.VMEM)
        dma = pltpu.SemaphoreType.DMA
        f32 = jnp.float32
        return pl.pallas_call(
            make_kernel(lat_count, lev_count, nf, levels, rows, lons, segs),
            out_shape=(
                pltpu.VMEM((nf, levels, rows, lons), f32),
                pltpu.VMEM((levels, rows, lons), f32),
                pltpu.VMEM((nf, levels, half, lons), f32),
            ),
            in_specs=[any_spec] * 5,
            out_specs=[vmem_spec] * 3,
            scratch_shapes=[
                pltpu.VMEM((nf, levels, rows, lons), f32),
                pltpu.VMEM((2, levels, rows, lons), f32),
                pltpu.VMEM((rows, lons), f32),
                pltpu.VMEM((2, nf, levels, 1, lons), f32),
                pltpu.VMEM((rows, lons), f32),
                pltpu.VMEM((lev_count - 1, rows, lons), f32),
                pltpu.VMEM((nf, levels, half, lons), f32),
                pltpu.VMEM((5, rows, LANES), f32),
                pltpu.SMEM((rows,), jnp.int32),
                pltpu.SMEM((levels,), f32),
                pltpu.SMEM((rows,), jnp.int32),
                dma((nf * levels,)),
                dma((2, levels)),
                dma((3,)),
                dma((2,)),
                dma((2,)),
                dma((lev_count - 1,)),
                dma((lev_count - 1,)),
                dma((nf * levels, segs)),
                dma((nf * levels, segs)),
            ],
            compiler_params=pltpu.CompilerParams(
                collective_id=0, has_side_effects=True, vmem_limit_bytes=40 * 1024 * 1024
            ),
            name="step",
        )(fields, velocity, surface, thickness, row_owner)

    in_specs = (
        P(None, "lev", "lat", None),
        P(None, "lev", "lat", None),
        P("lat", None),
        P("lev"),
        P("lat"),
    )
    out_specs = (P(None, "lev", "lat", None), P("lev", "lat", None), P(None, "lev", "lat", None))
    return jax.shard_map(local, mesh=mesh, in_specs=in_specs, out_specs=out_specs, check_vma=False)
```

time: 434 us -> 416 us (0.959)
  Pallas kernels: 0 us -> 406 us
  other arithmetic: 170 us -> 0 us
  waiting for transfers between devices: 126 us -> 0 us
  local copies, waits for them, and re-layouts: 114 us -> 8.03 us
  starting transfers between devices: 16.6 us -> 0 us
    pallas_call x0 -> x1, Pallas kernels: none -> 406 us  [local(): pl.pallas_call(make_kernel(lat_count, lev_count, nf, levels, rows, lons,...]
    ppermute x6 -> x0, waiting for transfers between devices: 126 us -> none  [the longest x4 126 us: shifted(): lax.ppermute(array, axis, [(i, (i + by) % size) for i in range(size)])]
    mul x11 -> x0, other arithmetic: 84.9 us -> none  [the longest x8 82.1 us: smooth(): fluxes = strength * (slopes - limited)]
    slice x44 -> x0, local copies, waits for them, and re-layouts: 59.2 us -> none  [the longest x16 16.9 us: smooth(): jnp.roll(slopes, 1, axis=-1)]
    sub x15 -> x0, other arithmetic: 30.5 us -> none  [the longest x7 18 us: smooth(): state = state + fluxes - jnp.roll(fluxes, 1, axis=-1)]
    gather x6 -> x0, local copies, waits for them, and re-layouts: 25.2 us -> none  [the longest x2 10.4 us: take_rows(): jnp.take(source_data, source_rows, axis=2)]
    add x3 -> x0, other arithmetic: 21.4 us -> none  [the longest x1 20.1 us: advect(): result + diffuse_lat * metric * (cos_north * (north_rows - state) - cos_s...]
    select_n x11 -> x0, other arithmetic: 20.7 us -> none  [the longest x1 9.21 us: local(): jnp.where(kept_rows[:, None], jnp.take(polar_rows, kept_slot, axis=2), pl...]
  transfers between devices with their start and end apart: 7 -> 0, of which waited for: 2 -> 0; matrix products, arithmetic and copies ran while one was open for 16% -> 0% of each run, Pallas kernels for 0% -> 0%
where the time goes in v1:
time: 416 us; the launch traced here: 414 us
  Pallas kernels  406 us (98%)
  local copies, waits for them, and re-layouts  8.03 us (2%)
    pallas_call x1, Pallas kernels, local(): pl.pallas_call(make_kernel(lat_count, lev_count, nf, levels, rows, lons,...  406 us

profile of v1, /device:TPU:38, one launch (start us, length us, event | category | flops | bytes accessed | tf_op | source)
XLA Modules:
  0.0 414.3 jit_solution(16804131122004251275)
XLA Ops:
  0.6 0.0 copy-start
  0.6 1.0 copy-done
  1.7 0.0 copy-start.1
  1.7 0.7 copy-done.1
  2.3 0.0 copy-start.2
  2.3 0.7 copy-done.2
  3.0 405.6 %step.1 = (f32[3,4,32,4096]{3,2,1,0:T(8,128)S(1)}, f32[4,32,4096]{2,1,0:T(8,128)S(1)}, f32[3,4,16,4096]{3,2,1,0:T(8,128)S(1)}) custom-call(f32[3,4,32,4096]{3,2,1,0:T(8,128)} %fields.1, f32[2,4,32,4096]{3,2,1,0:T(8,128)} %velocity.1, f32[32,4096]{1,0:T(8,128)S(1)} %copy-done, f32[4]{0:T(128)S(1)} %copy-done.1, s32[32]{0:T(128)S(1)} %copy-done.2), custom_call_target="tpu_custom_call" | custom-call | tf_op jit(solution)/shard_map/step/pallas_call | solution.py:371
  408.6 2.7 copy.11
  411.3 1.3 copy.12
  412.7 1.7 copy.13
Async XLA Ops:
  0.6 1.0 copy-start
  1.7 0.7 copy-start.1
  2.3 0.7 copy-start.2

commit v2 on v1

v2 whole, which is shorter than its diff:
```python
import math

import jax
import jax.numpy as jnp
from jax import lax
from jax.experimental import pallas as pl
from jax.experimental.pallas import tpu as pltpu
from jax.sharding import PartitionSpec as P

PASSES = 8
PAD = 2 * PASSES
SLACK = 32
STEPS = 68
LANES = 128
SUBS = 8
CHUNK = 512
MESH = pl.DeviceIdType.MESH

courant_lon = 0.3
courant_lat = 0.3
diffuse_lon = 0.04
diffuse_lat = 0.08
base_temp = 3.0


def strength_of(row_ids, all_rows):
    cos_mid = jnp.cos(-0.5 * math.pi + (row_ids + 0.5) * (math.pi / all_rows))
    polar = (row_ids < all_rows // 4) | (row_ids >= all_rows - all_rows // 4)
    return jnp.where(polar, 0.05 + 0.2 * (1.0 - cos_mid / math.cos(0.25 * math.pi)), 0.0)


def make_kernel(lat_count, lev_count, nf, levels, rows, lons):
    half = rows // 2
    slabs = nf * levels
    groups = rows // SUBS
    all_rows = rows * lat_count
    spacing = math.pi / all_rows
    shift = lat_count // 2
    quarter = lat_count // 4
    blocks = lons // LANES
    per = CHUNK // LANES
    chunks = lons // CHUNK
    segment = lons // SUBS
    per_segment = segment // LANES
    length = segment + 2 * PAD + SLACK
    last_q = nf - 1

    def kernel(
        fields, velocity, surface, thickness, row_owner,
        new_fields, geo, polar_rows,
        cells, wind, ground, halo, below, columns, packed, landed, front, back,
        tables, factor, factor_out, owners, thick, slots,
        in_sem, wind_sem, small_sem, halo_send, halo_recv, col_send, col_recv, row_send, row_recv,
        factor_sem,
    ):
        me = lax.axis_index("lat")
        lev = lax.axis_index("lev")
        polar = (me < quarter) | (me >= lat_count - quarter)
        plain = jnp.logical_not(polar)
        partner = lax.rem(me + shift, lat_count)

        def cell_copy(q, k):
            return pltpu.make_async_copy(fields.at[q, k], cells.at[q, k], in_sem.at[q, k])

        def wind_copy(k, part):
            return pltpu.make_async_copy(velocity.at[part, k], wind.at[part, k], wind_sem.at[part, k])

        own_copy = pltpu.make_async_copy(row_owner, owners, small_sem.at[0])
        thick_copy = pltpu.make_async_copy(thickness, thick, small_sem.at[1])
        ground_copy = pltpu.make_async_copy(surface, ground, small_sem.at[2])

        barrier = pltpu.get_barrier_semaphore()
        for by in (shift, 1, lat_count - 1):
            pl.semaphore_signal(
                barrier, inc=1, device_id={"lat": lax.rem(me + by, lat_count)}, device_id_type=MESH
            )
        for by in range(1, lev_count):
            pl.semaphore_signal(
                barrier, inc=1, device_id={"lev": lax.rem(lev + by, lev_count)}, device_id_type=MESH
            )

        for q in range(nf):
            for k in reversed(range(levels)):
                cell_copy(q, k).start()
                if q == 0:
                    wind_copy(k, 0).start()
                    wind_copy(k, 1).start()
                    if k == levels - 1:
                        own_copy.start()
                        thick_copy.start()
        ground_copy.start()

        row_ids = (me * rows + lax.broadcasted_iota(jnp.int32, (rows, LANES), 0)).astype(jnp.float32)
        lat_mid = -0.5 * math.pi + (row_ids + 0.5) * spacing
        metric = 1.0 / jnp.maximum(jnp.cos(lat_mid), 0.25)
        to_north = diffuse_lat * metric * jnp.cos(lat_mid + 0.5 * spacing)
        to_south = diffuse_lat * metric * jnp.cos(lat_mid - 0.5 * spacing)
        to_side = diffuse_lon * metric * metric
        tables[0] = 0.5 * courant_lon * metric
        tables[1] = to_side
        tables[2] = to_north
        tables[3] = to_south
        tables[4] = 1.0 - 2.0 * to_side - to_north - to_south

        lane = lax.broadcasted_iota(jnp.int32, (SUBS, LANES), 1)
        for place in range(SLACK):
            at = (segment + 2 * PAD + place) * SUBS
            front[at : at + SUBS, :] = jnp.zeros((SUBS, LANES), jnp.float32)

        own_copy.wait()
        thick_copy.wait()
        sent_from = [jnp.int32(0)] * half
        kept_from = [jnp.int32(0)] * half
        sent = jnp.int32(0)
        for row in range(rows):
            away = (owners[row] != me).astype(jnp.int32)
            kept = row - sent
            for slot in range(max(0, row - half), min(half, row + 1)):
                sent_from[slot] = jnp.where((away == 1) & (sent == slot), row, sent_from[slot])
                kept_from[slot] = jnp.where((away == 0) & (kept == slot), row, kept_from[slot])
            sent = sent + away
        for slot in range(half):
            slots[slot] = sent_from[slot]
            slots[half + slot] = kept_from[slot]

        @pl.when(polar)
        def _():
            here = lax.rem(lane, rows)
            away = jnp.zeros((SUBS, LANES), jnp.int32)
            slot_of = lax.rem(lane, half)
            for slot in range(half):
                away = jnp.where(slot_of == slot, slots[slot], away)
            factor[...] = strength_of((me * rows + here).astype(jnp.float32), all_rows)
            factor_out[...] = strength_of((me * rows + away).astype(jnp.float32), all_rows)

        pl.semaphore_wait(barrier, 3 + lev_count - 1)

        north_copy = pltpu.make_async_remote_copy(
            src_ref=fields.at[:, :, rows - 1 : rows, :], dst_ref=halo.at[0],
            send_sem=halo_send.at[0], recv_sem=halo_recv.at[0],
            device_id={"lat": lax.rem(me + 1, lat_count)}, device_id_type=MESH,
        )
        south_copy = pltpu.make_async_remote_copy(
            src_ref=fields.at[:, :, 0:1, :], dst_ref=halo.at[1],
            send_sem=halo_send.at[1], recv_sem=halo_recv.at[1],
            device_id={"lat": lax.rem(me + lat_count - 1, lat_count)}, device_id_type=MESH,
        )
        own_south = pltpu.make_async_copy(fields.at[:, :, 0:1, :], halo.at[0], halo_recv.at[0])
        own_north = pltpu.make_async_copy(fields.at[:, :, rows - 1 : rows, :], halo.at[1], halo_recv.at[1])
        first = me == 0
        last = me == lat_count - 1

        @pl.when(jnp.logical_not(last))
        def _():
            north_copy.start()

        @pl.when(jnp.logical_not(first))
        def _():
            south_copy.start()

        @pl.when(first)
        def _():
            own_south.start()

        @pl.when(last)
        def _():
            own_north.start()

        factor_copy = pltpu.make_async_remote_copy(
            src_ref=factor_out, dst_ref=factor, send_sem=factor_sem.at[0], recv_sem=factor_sem.at[1],
            device_id={"lat": partner}, device_id_type=MESH,
        )

        def early_copy(q, k):
            return pltpu.make_async_remote_copy(
                src_ref=packed.at[q, k], dst_ref=landed.at[q, k],
                send_sem=row_send.at[q, k], recv_sem=row_recv.at[q, k],
                device_id={"lat": partner}, device_id_type=MESH,
            )

        def late_copy(k):
            return pltpu.make_async_remote_copy(
                src_ref=packed.at[last_q, k], dst_ref=polar_rows.at[last_q, k],
                send_sem=row_send.at[last_q, k], recv_sem=row_recv.at[last_q, k],
                device_id={"lat": partner}, device_id_type=MESH,
            )

        def col_copy(by):
            return pltpu.make_async_remote_copy(
                src_ref=below, dst_ref=columns.at[by - 1],
                send_sem=col_send.at[by - 1], recv_sem=col_recv.at[by - 1],
                device_id={"lev": lax.rem(lev + lev_count - by, lev_count)}, device_id_type=MESH,
            )

        @pl.when(polar)
        def _():
            factor_copy.start()

        @pl.when(first)
        def _():
            own_south.wait()

        @pl.when(jnp.logical_not(first))
        def _():
            north_copy.wait_recv()

        @pl.when(last)
        def _():
            own_north.wait()

        @pl.when(jnp.logical_not(last))
        def _():
            south_copy.wait_recv()

        sub = lax.broadcasted_iota(jnp.int32, (SUBS, CHUNK), 0)

        def advect_chunk(q, k, part):
            cols = pl.ds(pl.multiple_of(part * CHUNK, LANES), CHUNK)
            left = pl.ds(pl.multiple_of(lax.rem(part * per + blocks - 1, blocks) * LANES, LANES), LANES)
            right = pl.ds(pl.multiple_of(lax.rem((part + 1) * per, blocks) * LANES, LANES), LANES)

            def spread(table, group):
                one = tables[table, group * SUBS : (group + 1) * SUBS, :]
                return jnp.concatenate([one] * per, axis=1)

            state = [cells[q, k, g * SUBS : (g + 1) * SUBS, cols] for g in range(groups)]
            up = [pltpu.roll(one, SUBS - 1, 0) for one in state]
            up.append(jnp.broadcast_to(halo[1, q, k, :, cols], (SUBS, CHUNK)))
            down = [jnp.broadcast_to(halo[0, q, k, :, cols], (SUBS, CHUNK))]
            down += [pltpu.roll(one, 1, 0) for one in state]
            for g in range(groups):
                span = pl.ds(g * SUBS, SUBS)
                wide = CHUNK + LANES
                east = pltpu.roll(jnp.concatenate([state[g], cells[q, k, span, right]], axis=1), wide - 1, 1)
                west = pltpu.roll(jnp.concatenate([cells[q, k, span, left], state[g]], axis=1), 1, 1)
                east, west = east[:, :CHUNK], west[:, LANES:]
                north = jnp.where(sub == SUBS - 1, up[g + 1], up[g])
                south = jnp.where(sub == 0, down[g], down[g + 1])
                along = spread(0, g) * wind[0, k, span, cols]
                across = (0.5 * courant_lat) * wind[1, k, span, cols]
                side = spread(1, g)
                result = (
                    spread(4, g) * state[g]
                    + ((side - along) * east + (side + along) * west)
                    + ((spread(2, g) - across) * north + (spread(3, g) + across) * south)
                )
                new_fields[q, k, span, cols] = result
                if isinstance(q, int) and q == 0:
                    weight = (base_temp + result) * thick[k]
                    so_far = jnp.where(k == levels - 1, 0.0, below[span, cols])
                    geo[k, span, cols] = so_far + 0.5 * weight
                    below[span, cols] = so_far + weight

        def advect_level(q, k):
            def one(part, carry):
                advect_chunk(q, k, part)
                return carry

            lax.fori_loop(0, chunks, one, 0)

        def pack(q, k):
            for slot in range(half):
                packed[q, k, slot : slot + 1, :] = new_fields[q, k, pl.ds(slots[slot], 1), :]

        def keep(q, k):
            for slot in range(half):
                polar_rows[q, k, slot : slot + 1, :] = new_fields[q, k, pl.ds(slots[half + slot], 1), :]

        def first_field(index, carry):
            k = levels - 1 - index
            cell_copy(0, k).wait()
            wind_copy(k, 0).wait()
            wind_copy(k, 1).wait()
            advect_level(0, k)

            @pl.when(polar)
            def _():
                pack(0, k)
                early_copy(0, k).start()

            return carry

        lax.fori_loop(0, levels, first_field, 0)

        for by in range(1, lev_count):
            @pl.when(lev >= by)
            def _():
                col_copy(by).start()

        def next_field(index, carry):
            q = 1 + index // levels
            k = levels - 1 - lax.rem(index, levels)
            cell_copy(q, k).wait()
            advect_level(q, k)

            @pl.when(polar & (q < last_q))
            def _():
                pack(q, k)
                early_copy(q, k).start()

            return carry

        lax.fori_loop(0, slabs - levels, next_field, 0)

        def place_of(block):
            return lax.rem(block, per_segment) * LANES + PAD, block // per_segment

        def run(place):
            return pl.ds(pl.multiple_of(place * SUBS, SUBS), SUBS)

        def put_block(block, values):
            start, which = place_of(block)
            turned = values.T
            for v in range(LANES // SUBS):
                front[pl.ds((start + SUBS * v) * SUBS + which, SUBS, stride=SUBS), :] = turned[
                    SUBS * v : SUBS * (v + 1), :
                ]

        def get_block(block):
            start, which = place_of(block)
            return jnp.concatenate(
                [
                    front[pl.ds((start + SUBS * v) * SUBS + which, SUBS, stride=SUBS), :]
                    for v in range(LANES // SUBS)
                ],
                axis=0,
            ).T

        def cols_of(block):
            return pl.ds(pl.multiple_of(block * LANES, LANES), LANES)

        def one_pass(source, target, start, strength):
            def flux_of(west, slope, east):
                least = jnp.minimum(jnp.maximum(west, east), 0.0)
                most = jnp.maximum(jnp.minimum(west, east), 0.0)
                return strength * (slope - jnp.minimum(jnp.maximum(slope, least), most))

            def steps(index, state):
                cell, ahead, west, slope, inflow = state
                base = start + index * STEPS
                for j in range(STEPS):
                    beyond = source[run(base + j + 2), :]
                    east = beyond - ahead
                    outflow = flux_of(west, slope, east)
                    target[run(base + j), :] = cell + (outflow - inflow)
                    cell, ahead, west, slope, inflow = ahead, beyond, slope, east, outflow
                return cell, ahead, west, slope, inflow

            near = [source[run(start - 2 + j), :] for j in range(4)]
            slopes = [near[j + 1] - near[j] for j in range(3)]
            inflow = flux_of(slopes[0], slopes[1], slopes[2])
            lax.fori_loop(
                0, (length - SLACK) // STEPS, steps, (near[2], near[3], slopes[1], slopes[2], inflow)
            )

        def all_passes():
            for j in range(PAD):
                front[j * SUBS : (j + 1) * SUBS, :] = pltpu.roll(
                    front[(segment + j) * SUBS : (segment + j + 1) * SUBS, :], 1, 0
                )
                end = (PAD + segment + j) * SUBS
                front[end : end + SUBS, :] = pltpu.roll(
                    front[(PAD + j) * SUBS : (PAD + j + 1) * SUBS, :], SUBS - 1, 0
                )
            strength = factor[...]

            def pair(index, carry):
                one_pass(front, back, 2 + 4 * index, strength)
                one_pass(back, front, 4 + 4 * index, strength)
                return carry

            lax.fori_loop(0, PASSES // 2, pair, 0)

        @pl.when(plain)
        def _():
            factor_copy.wait_recv()

        def job(index, carry):
            q = lax.rem(index + last_q, nf)

            @pl.when(polar)
            def _():
                def fill(block, carry):
                    values = new_fields[q, :, :, cols_of(block)]
                    put_block(block, values.reshape(LANES, LANES))
                    return carry

                lax.fori_loop(0, blocks, fill, 0)

            @pl.when(plain & (index < last_q))
            def _():
                def heard(k, carry):
                    early_copy(index, levels - 1 - k).wait_recv()
                    return carry

                lax.fori_loop(0, levels, heard, 0)

                def fill(block, carry):
                    values = landed[index, :, :, cols_of(block)].reshape(levels * half, LANES)
                    put_block(block, jnp.concatenate([values, values], axis=0))
                    return carry

                lax.fori_loop(0, blocks, fill, 0)

            @pl.when(polar | (index < last_q))
            def _():
                all_passes()

            @pl.when(polar)
            def _():
                def spill(block, carry):
                    new_fields[q, :, :, cols_of(block)] = get_block(block).reshape(levels, rows, LANES)
                    return carry

                lax.fori_loop(0, blocks, spill, 0)

                @pl.when(index == 0)
                def _():
                    def send(k, carry):
                        pack(last_q, k)
                        late_copy(k).start()
                        return carry

                    lax.fori_loop(0, levels, send, 0)

                def hold(k, carry):
                    keep(q, k)
                    return carry

                lax.fori_loop(0, levels, hold, 0)

            @pl.when(plain & (index < last_q))
            def _():
                def spill(block, carry):
                    values = get_block(block)[: levels * half, :]
                    polar_rows[index, :, :, cols_of(block)] = values.reshape(levels, half, LANES)
                    return carry

                lax.fori_loop(0, blocks, spill, 0)

            return carry

        lax.fori_loop(0, nf, job, 0)

        ground_copy.wait()
        for by in range(1, lev_count):
            @pl.when(lev + by < lev_count)
            def _():
                col_copy(by).wait_recv()

        def finish(index, carry):
            span = pl.ds(pl.multiple_of(index * SUBS, SUBS), SUBS)
            outside = ground[span, :]
            for by in range(1, lev_count):
                outside = outside + jnp.where(lev + by < lev_count, columns[by - 1, span, :], 0.0)
            for k in range(levels):
                geo[k, span, :] = geo[k, span, :] + outside
            return carry

        lax.fori_loop(0, groups, finish, 0)

        for by in range(1, lev_count):
            @pl.when(lev >= by)
            def _():
                col_copy(by).wait_send()

        @pl.when(jnp.logical_not(last))
        def _():
            north_copy.wait_send()

        @pl.when(jnp.logical_not(first))
        def _():
            south_copy.wait_send()

        @pl.when(polar)
        def _():
            factor_copy.wait_send()
            for q in range(last_q):
                for k in range(levels):
                    early_copy(q, k).wait_send()
            for k in range(levels):
                late_copy(k).wait_send()

        @pl.when(plain)
        def _():
            for k in range(levels):
                late_copy(k).wait_recv()

    return kernel


def write_out(new_fields, geo, polar_rows, new_fields_out, geo_out, polar_rows_out, sem):
    copies = [
        pltpu.make_async_copy(new_fields, new_fields_out, sem.at[0]),
        pltpu.make_async_copy(geo, geo_out, sem.at[1]),
        pltpu.make_async_copy(polar_rows, polar_rows_out, sem.at[2]),
    ]
    for copy in copies:
        copy.start()
    for copy in copies:
        copy.wait()


def solution(mesh):
    lat_count, lev_count = mesh.shape["lat"], mesh.shape["lev"]

    def local(fields, velocity, surface, thickness, row_owner):
        nf, levels, rows, lons = fields.shape
        half = rows // 2
        length = lons // SUBS + 2 * PAD + SLACK
        hbm_spec = pl.BlockSpec(memory_space=pltpu.HBM)
        vmem_spec = pl.BlockSpec(memory_space=pltpu.VMEM)
        dma = pltpu.SemaphoreType.DMA
        f32 = jnp.float32
        shapes = ((nf, levels, rows, lons), (levels, rows, lons), (nf, levels, half, lons))
        held = pl.pallas_call(
            make_kernel(lat_count, lev_count, nf, levels, rows, lons),
            out_shape=tuple(pltpu.VMEM(shape, f32) for shape in shapes),
            in_specs=[hbm_spec] * 5,
            out_specs=[vmem_spec] * 3,
            scratch_shapes=[
                pltpu.VMEM((nf, levels, rows, lons), f32),
                pltpu.VMEM((2, levels, rows, lons), f32),
                pltpu.VMEM((rows, lons), f32),
                pltpu.VMEM((2, nf, levels, 1, lons), f32),
                pltpu.VMEM((rows, lons), f32),
                pltpu.VMEM((lev_count - 1, rows, lons), f32),
                pltpu.VMEM((nf, levels, half, lons), f32),
                pltpu.VMEM((nf - 1, levels, half, lons), f32),
                pltpu.VMEM((length * SUBS, LANES), f32),
                pltpu.VMEM((length * SUBS, LANES), f32),
                pltpu.VMEM((5, rows, LANES), f32),
                pltpu.VMEM((SUBS, LANES), f32),
                pltpu.VMEM((SUBS, LANES), f32),
                pltpu.SMEM((rows,), jnp.int32),
                pltpu.SMEM((levels,), f32),
                pltpu.SMEM((rows,), jnp.int32),
                dma((nf, levels)),
                dma((2, levels)),
                dma((3,)),
                dma((2,)),
                dma((2,)),
                dma((lev_count - 1,)),
                dma((lev_count - 1,)),
                dma((nf, levels)),
                dma((nf, levels)),
                dma((2,)),
            ],
            compiler_params=pltpu.CompilerParams(
                collective_id=0, has_side_effects=True, vmem_limit_bytes=40 * 1024 * 1024
            ),
            name="step",
        )(fields, velocity, surface, thickness, row_owner)
        return pl.pallas_call(
            write_out,
            out_shape=tuple(jax.ShapeDtypeStruct(shape, f32) for shape in shapes),
            in_specs=[pl.BlockSpec(memory_space=pl.ANY)] * 3,
            out_specs=[hbm_spec] * 3,
            scratch_shapes=[dma((3,))],
            compiler_params=pltpu.CompilerParams(vmem_limit_bytes=1024 * 1024),
            name="write",
        )(*held)

    in_specs = (
        P(None, "lev", "lat", None),
        P(None, "lev", "lat", None),
        P("lat", None),
        P("lev"),
        P("lat"),
    )
    out_specs = (P(None, "lev", "lat", None), P("lev", "lat", None), P(None, "lev", "lat", None))
    return jax.shard_map(local, mesh=mesh, in_specs=in_specs, out_specs=out_specs, check_vma=False)
```

time: 416 us -> 89 us (0.21)
  the two profiles are of different devices: /device:TPU:38 before, /device:TPU:32 now
where the time goes in v2:
time: 89 us; the launch traced here: 88.8 us
  Pallas kernels  85.8 us (96%)
  local copies, waits for them, and re-layouts  2.34 us (3%)
    pallas_call x1, Pallas kernels, local(): pl.pallas_call(make_kernel(lat_count, lev_count, nf, levels, rows, lons),...  81.4 us
    pallas_call x1, Pallas kernels, local(): pl.pallas_call(write_out, out_shape=tuple((jax.ShapeDtypeStruct(shape, f3...  4.39 us
    unnamed x6, local copies, waits for them, and re-layouts  2.34 us

profile of v2, /device:TPU:32, one launch (start us, length us, event | category | flops | bytes accessed | tf_op | source)
XLA Modules:
  0.0 88.8 jit_solution(14105604796395799922)
XLA Ops:
  0.6 0.0 copy-start
  0.6 1.0 %copy-done = f32[32,4096]{1,0:T(8,128)S(1)} copy-done((f32[32,4096]{1,0:T(8,128)S(1)}, f32[32,4096]{1,0:T(8,128)}, u32[]{:S(2)}) %copy-start) | copy-done | bytes 524312
  1.7 0.0 copy-start.1
  1.7 0.7 copy-done.1
  2.3 0.0 copy-start.2
  2.3 0.7 copy-done.2
  3.0 81.4 %step.1 = (f32[3,4,32,4096]{3,2,1,0:T(8,128)S(1)}, f32[4,32,4096]{2,1,0:T(8,128)S(1)}, f32[3,4,16,4096]{3,2,1,0:T(8,128)S(1)}) custom-call(f32[3,4,32,4096]{3,2,1,0:T(8,128)} %fields.1, f32[2,4,32,4096]{3,2,1,0:T(8,128)} %velocity.1, f32[32,4096]{1,0:T(8,128)S(1)} %copy-done, f32[4]{0:T(128)S(1)} %copy-done.1, s32[32]{0:T(128)S(1)} %copy-done.2), custom_call_target="tpu_custom_call" | custom-call | tf_op jit(solution)/shard_map/step/pallas_call | solution.py:516
  84.4 4.4 %write.1 = (f32[3,4,32,4096]{3,2,1,0:T(8,128)}, f32[4,32,4096]{2,1,0:T(8,128)}, f32[3,4,16,4096]{3,2,1,0:T(8,128)}) custom-call(f32[3,4,32,4096]{3,2,1,0:T(8,128)S(1)} %get-tuple-element.6.new_fields, f32[4,32,4096]{2,1,0:T(8,128)S(1)} %get-tuple-element.7.geo, f32[3,4,16,4096]{3,2,1,0:T(8,128)S(1)} %get-tuple-element.8.polar_rows), custom_call_target="tpu_custom_call" | custom-call | tf_op jit(solution)/shard_map/write/pallas_call | solution.py:554
Async XLA Ops:
  0.6 1.0 %copy-start = (f32[32,4096]{1,0:T(8,128)S(1)}, f32[32,4096]{1,0:T(8,128)}, u32[]{:S(2)}) copy-start(f32[32,4096]{1,0:T(8,128)} %surface.1) | copy-start | bytes 1572868
  1.7 0.7 copy-start.1
  2.3 0.7 copy-start.2

commit v3 on v2

--- a/solution.py
+++ b/solution.py
@@ -14,6 +14,7 @@
 LANES = 128
 SUBS = 8
 CHUNK = 512
+UNROLL = 8
 MESH = pl.DeviceIdType.MESH
 
 courant_lon = 0.3
@@ -44,14 +45,15 @@
     per_segment = segment // LANES
     length = segment + 2 * PAD + SLACK
     last_q = nf - 1
+    order = list(range(1, half - 1)) + [0, half - 1]
 
     def kernel(
         fields, velocity, surface, thickness, row_owner,
         new_fields, geo, polar_rows,
         cells, wind, ground, halo, below, columns, packed, landed, front, back,
         tables, factor, factor_out, owners, thick, slots,
-        in_sem, wind_sem, small_sem, halo_send, halo_recv, col_send, col_recv, row_send, row_recv,
-        factor_sem,
+        in_sem, wind_sem, small_sem, halo_send, halo_recv, col_send, col_recv, early_send,
+        early_recv, late_send, late_recv, factor_sem,
     ):
         me = lax.axis_index("lat")
         lev = lax.axis_index("lev")
@@ -109,31 +111,20 @@
 
         own_copy.wait()
         thick_copy.wait()
-        sent_from = [jnp.int32(0)] * half
-        kept_from = [jnp.int32(0)] * half
-        sent = jnp.int32(0)
+        sent, kept = [], []
         for row in range(rows):
             away = (owners[row] != me).astype(jnp.int32)
-            kept = row - sent
-            for slot in range(max(0, row - half), min(half, row + 1)):
-                sent_from[slot] = jnp.where((away == 1) & (sent == slot), row, sent_from[slot])
-                kept_from[slot] = jnp.where((away == 0) & (kept == slot), row, kept_from[slot])
-            sent = sent + away
-        for slot in range(half):
-            slots[slot] = sent_from[slot]
-            slots[half + slot] = kept_from[slot]
-
-        @pl.when(polar)
-        def _():
-            here = lax.rem(lane, rows)
-            away = jnp.zeros((SUBS, LANES), jnp.int32)
-            slot_of = lax.rem(lane, half)
+            sent.append(away + (sent[-1] if row else 0))
+            kept.append(row + 1 - sent[-1])
+
+        def fill_slots(counts, base):
             for slot in range(half):
-                away = jnp.where(slot_of == slot, slots[slot], away)
-            factor[...] = strength_of((me * rows + here).astype(jnp.float32), all_rows)
-            factor_out[...] = strength_of((me * rows + away).astype(jnp.float32), all_rows)
-
-        pl.semaphore_wait(barrier, 3 + lev_count - 1)
+                place = jnp.int32(slot)
+                for row in range(slot, slot + half):
+                    place = place + (counts[row] <= slot).astype(jnp.int32)
+                slots[base + slot] = place
+
+        fill_slots(sent, 0)
 
         north_copy = pltpu.make_async_remote_copy(
             src_ref=fields.at[:, :, rows - 1 : rows, :], dst_ref=halo.at[0],
@@ -150,38 +141,23 @@
         first = me == 0
         last = me == lat_count - 1
 
-        @pl.when(jnp.logical_not(last))
-        def _():
-            north_copy.start()
-
-        @pl.when(jnp.logical_not(first))
-        def _():
-            south_copy.start()
-
-        @pl.when(first)
-        def _():
-            own_south.start()
-
-        @pl.when(last)
-        def _():
-            own_north.start()
-
         factor_copy = pltpu.make_async_remote_copy(
             src_ref=factor_out, dst_ref=factor, send_sem=factor_sem.at[0], recv_sem=factor_sem.at[1],
             device_id={"lat": partner}, device_id_type=MESH,
         )
 
-        def early_copy(q, k):
+        def early_copy(q, k, part):
+            span = pl.ds(part * SUBS, SUBS)
             return pltpu.make_async_remote_copy(
-                src_ref=packed.at[q, k], dst_ref=landed.at[q, k],
-                send_sem=row_send.at[q, k], recv_sem=row_recv.at[q, k],
+                src_ref=packed.at[q, k, span], dst_ref=landed.at[q, k, span],
+                send_sem=early_send.at[q, k, part], recv_sem=early_recv.at[q, k, part],
                 device_id={"lat": partner}, device_id_type=MESH,
             )
 
         def late_copy(k):
             return pltpu.make_async_remote_copy(
                 src_ref=packed.at[last_q, k], dst_ref=polar_rows.at[last_q, k],
-                send_sem=row_send.at[last_q, k], recv_sem=row_recv.at[last_q, k],
+                send_sem=late_send.at[k], recv_sem=late_recv.at[k],
                 device_id={"lat": partner}, device_id_type=MESH,
             )
 
@@ -192,29 +168,9 @@
                 device_id={"lev": lax.rem(lev + lev_count - by, lev_count)}, device_id_type=MESH,
             )
 
-        @pl.when(polar)
-        def _():
-            factor_copy.start()
-
-        @pl.when(first)
-        def _():
-            own_south.wait()
-
-        @pl.when(jnp.logical_not(first))
-        def _():
-            north_copy.wait_recv()
-
-        @pl.when(last)
-        def _():
-            own_north.wait()
-
-        @pl.when(jnp.logical_not(last))
-        def _():
-            south_copy.wait_recv()
-
         sub = lax.broadcasted_iota(jnp.int32, (SUBS, CHUNK), 0)
 
-        def advect_chunk(q, k, part):
+        def advect_chunk(q, k, part, edges):
             cols = pl.ds(pl.multiple_of(part * CHUNK, LANES), CHUNK)
             left = pl.ds(pl.multiple_of(lax.rem(part * per + blocks - 1, blocks) * LANES, LANES), LANES)
             right = pl.ds(pl.multiple_of(lax.rem((part + 1) * per, blocks) * LANES, LANES), LANES)
@@ -225,8 +181,12 @@
 
             state = [cells[q, k, g * SUBS : (g + 1) * SUBS, cols] for g in range(groups)]
             up = [pltpu.roll(one, SUBS - 1, 0) for one in state]
-            up.append(jnp.broadcast_to(halo[1, q, k, :, cols], (SUBS, CHUNK)))
-            down = [jnp.broadcast_to(halo[0, q, k, :, cols], (SUBS, CHUNK))]
+            if edges:
+                up.append(jnp.broadcast_to(halo[1, q, k, :, cols], (SUBS, CHUNK)))
+                down = [jnp.broadcast_to(halo[0, q, k, :, cols], (SUBS, CHUNK))]
+            else:
+                up.append(state[groups - 1])
+                down = [state[0]]
             down += [pltpu.roll(one, 1, 0) for one in state]
             for g in range(groups):
                 span = pl.ds(g * SUBS, SUBS)
@@ -245,58 +205,164 @@
                     + ((spread(2, g) - across) * north + (spread(3, g) + across) * south)
                 )
                 new_fields[q, k, span, cols] = result
-                if isinstance(q, int) and q == 0:
-                    weight = (base_temp + result) * thick[k]
-                    so_far = jnp.where(k == levels - 1, 0.0, below[span, cols])
-                    geo[k, span, cols] = so_far + 0.5 * weight
-                    below[span, cols] = so_far + weight
-
-        def advect_level(q, k):
+
+        def advect_level(q, k, edges):
             def one(part, carry):
-                advect_chunk(q, k, part)
+                advect_chunk(q, k, part, edges)
                 return carry
 
             lax.fori_loop(0, chunks, one, 0)
 
-        def pack(q, k):
-            for slot in range(half):
-                packed[q, k, slot : slot + 1, :] = new_fields[q, k, pl.ds(slots[slot], 1), :]
+        def pack(q, k, chosen, start=0):
+            for place, slot in enumerate(chosen):
+                packed[q, k, start + place : start + place + 1, :] = new_fields[
+                    q, k, pl.ds(slots[slot], 1), :
+                ]
 
         def keep(q, k):
             for slot in range(half):
                 polar_rows[q, k, slot : slot + 1, :] = new_fields[q, k, pl.ds(slots[half + slot], 1), :]
 
-        def first_field(index, carry):
-            k = levels - 1 - index
+        def first_level(k):
             cell_copy(0, k).wait()
             wind_copy(k, 0).wait()
             wind_copy(k, 1).wait()
-            advect_level(0, k)
+            advect_level(0, k, False)
 
             @pl.when(polar)
             def _():
-                pack(0, k)
-                early_copy(0, k).start()
+                pack(0, k, order[:SUBS])
+
+        first_level(levels - 1)
+        pl.semaphore_wait(barrier, 3 + lev_count - 1)
+
+        @pl.when(polar)
+        def _():
+            early_copy(0, levels - 1, 0).start()
+
+        @pl.when(jnp.logical_not(last))
+        def _():
+            north_copy.start()
+
+        @pl.when(jnp.logical_not(first))
+        def _():
+            south_copy.start()
+
+        @pl.when(first)
+        def _():
+            own_south.start()
+
+        @pl.when(last)
+        def _():
+            own_north.start()
+
+        def other_levels(index, carry):
+            k = levels - 2 - index
+            first_level(k)
+
+            @pl.when(polar)
+            def _():
+                early_copy(0, k, 0).start()
 
             return carry
 
-        lax.fori_loop(0, levels, first_field, 0)
+        lax.fori_loop(0, levels - 1, other_levels, 0)
+
+        @pl.when(polar)
+        def _():
+            here = lax.rem(lane, rows)
+            away = jnp.zeros((SUBS, LANES), jnp.int32)
+            slot_of = lax.rem(lane, half)
+            for place, slot in enumerate(order):
+                away = jnp.where(slot_of == place, slots[slot], away)
+            factor[...] = strength_of((me * rows + here).astype(jnp.float32), all_rows)
+            factor_out[...] = strength_of((me * rows + away).astype(jnp.float32), all_rows)
+
+        @pl.when(polar)
+        def _():
+            factor_copy.start()
+
+        @pl.when(first)
+        def _():
+            own_south.wait()
+
+        @pl.when(jnp.logical_not(first))
+        def _():
+            north_copy.wait_recv()
+
+        @pl.when(last)
+        def _():
+            own_north.wait()
+
+        @pl.when(jnp.logical_not(last))
+        def _():
+            south_copy.wait_recv()
+
+        def mend_edges(k, part):
+            cols = pl.ds(pl.multiple_of(part * CHUNK, LANES), CHUNK)
+            for side, group, line, sign in ((0, 0, 0, 1.0), (1, groups - 1, SUBS - 1, -1.0)):
+                span = pl.ds(group * SUBS, SUBS)
+                table = tables[3 - side, span, :]
+                weight = (
+                    jnp.concatenate([table] * per, axis=1)
+                    + (sign * 0.5 * courant_lat) * wind[1, k, span, cols]
+                )
+                beyond = jnp.broadcast_to(halo[side, 0, k, :, cols], (SUBS, CHUNK))
+                change = weight * (beyond - cells[0, k, span, cols])
+                new_fields[0, k, span, cols] = new_fields[0, k, span, cols] + jnp.where(
+                    sub == line, change, 0.0
+                )
+
+        def mend_level(index, carry):
+            k = levels - 1 - index
+
+            def one(part, carry):
+                mend_edges(k, part)
+                return carry
+
+            lax.fori_loop(0, chunks, one, 0)
+
+            @pl.when(polar)
+            def _():
+                pack(0, k, order[SUBS:], SUBS)
+                early_copy(0, k, 1).start()
+
+            return carry
+
+        lax.fori_loop(0, levels, mend_level, 0)
+
+        def add_levels(index, carry):
+            cols = pl.ds(pl.multiple_of(index * CHUNK, LANES), CHUNK)
+            for group in range(groups):
+                span = pl.ds(group * SUBS, SUBS)
+                so_far = jnp.zeros((SUBS, CHUNK), jnp.float32)
+                for k in reversed(range(levels)):
+                    weight = (base_temp + new_fields[0, k, span, cols]) * thick[k]
+                    geo[k, span, cols] = so_far + 0.5 * weight
+                    so_far = so_far + weight
+                below[span, cols] = so_far
+            return carry
+
+        lax.fori_loop(0, chunks, add_levels, 0)
 
         for by in range(1, lev_count):
             @pl.when(lev >= by)
             def _():
                 col_copy(by).start()
+
+        fill_slots(kept, half)
 
         def next_field(index, carry):
             q = 1 + index // levels
             k = levels - 1 - lax.rem(index, levels)
             cell_copy(q, k).wait()
-            advect_level(q, k)
+            advect_level(q, k, True)
 
             @pl.when(polar & (q < last_q))
             def _():
-                pack(q, k)
-                early_copy(q, k).start()
+                pack(q, k, order)
+                for part in range(half // SUBS):
+                    early_copy(q, k, part).start()
 
             return carry
 
@@ -380,27 +446,30 @@
 
             @pl.when(polar)
             def _():
-                def fill(block, carry):
-                    values = new_fields[q, :, :, cols_of(block)]
-                    put_block(block, values.reshape(LANES, LANES))
+                def fill(index, carry):
+                    for block in (index * UNROLL + i for i in range(UNROLL)):
+                        values = new_fields[q, :, :, cols_of(block)]
+                        put_block(block, values.reshape(LANES, LANES))
                     return carry
 
-                lax.fori_loop(0, blocks, fill, 0)
+                lax.fori_loop(0, blocks // UNROLL, fill, 0)
 
             @pl.when(plain & (index < last_q))
             def _():
                 def heard(k, carry):
-                    early_copy(index, levels - 1 - k).wait_recv()
+                    for part in range(half // SUBS):
+                        early_copy(index, levels - 1 - k, part).wait_recv()
                     return carry
 
                 lax.fori_loop(0, levels, heard, 0)
 
-                def fill(block, carry):
-                    values = landed[index, :, :, cols_of(block)].reshape(levels * half, LANES)
-                    put_block(block, jnp.concatenate([values, values], axis=0))
+                def fill(place, carry):
+                    for block in (place * UNROLL + i for i in range(UNROLL)):
+                        values = landed[index, :, :, cols_of(block)].reshape(levels * half, LANES)
+                        put_block(block, jnp.concatenate([values, values], axis=0))
                     return carry
 
-                lax.fori_loop(0, blocks, fill, 0)
+                lax.fori_loop(0, blocks // UNROLL, fill, 0)
 
             @pl.when(polar | (index < last_q))
             def _():
@@ -408,16 +477,19 @@
 
             @pl.when(polar)
             def _():
-                def spill(block, carry):
-                    new_fields[q, :, :, cols_of(block)] = get_block(block).reshape(levels, rows, LANES)
+                def spill(place, carry):
+                    for block in (place * UNROLL + i for i in range(UNROLL)):
+                        new_fields[q, :, :, cols_of(block)] = get_block(block).reshape(
+                            levels, rows, LANES
+                        )
                     return carry
 
-                lax.fori_loop(0, blocks, spill, 0)
+                lax.fori_loop(0, blocks // UNROLL, spill, 0)
 
                 @pl.when(index == 0)
                 def _():
                     def send(k, carry):
-                        pack(last_q, k)
+                        pack(last_q, k, range(half))
                         late_copy(k).start()
                         return carry
 
@@ -431,12 +503,16 @@
 
             @pl.when(plain & (index < last_q))
             def _():
-                def spill(block, carry):
-                    values = get_block(block)[: levels * half, :]
-                    polar_rows[index, :, :, cols_of(block)] = values.reshape(levels, half, LANES)
+                def spill(place, carry):
+                    for block in (place * UNROLL + i for i in range(UNROLL)):
+                        values = get_block(block)
+                        for k in range(levels):
+                            one = values[k * half : (k + 1) * half, :]
+                            whole = jnp.concatenate([one[half - 2 : half - 1], one[: half - 2], one[half - 1 :]], axis=0)
+                            polar_rows[index, k, :, cols_of(block)] = whole
                     return carry
 
-                lax.fori_loop(0, blocks, spill, 0)
+                lax.fori_loop(0, blocks // UNROLL, spill, 0)
 
             return carry
 
@@ -477,7 +553,8 @@
             factor_copy.wait_send()
             for q in range(last_q):
                 for k in range(levels):
-                    early_copy(q, k).wait_send()
+                    for part in range(half // SUBS):
+                        early_copy(q, k, part).wait_send()
             for k in range(levels):
                 late_copy(k).wait_send()
 
@@ -490,11 +567,14 @@
 
 
 def write_out(new_fields, geo, polar_rows, new_fields_out, geo_out, polar_rows_out, sem):
-    copies = [
-        pltpu.make_async_copy(new_fields, new_fields_out, sem.at[0]),
-        pltpu.make_async_copy(geo, geo_out, sem.at[1]),
-        pltpu.make_async_copy(polar_rows, polar_rows_out, sem.at[2]),
-    ]
+    levels = geo.shape[0]
+    copies = []
+    for k in range(levels):
+        for q in range(new_fields.shape[0]):
+            copies.append((new_fields.at[q, k], new_fields_out.at[q, k]))
+            copies.append((polar_rows.at[q, k], polar_rows_out.at[q, k]))
+        copies.append((geo.at[k], geo_out.at[k]))
+    copies = [pltpu.make_async_copy(*pair, sem.at[i]) for i, pair in enumerate(copies)]
     for copy in copies:
         copy.start()
     for copy in copies:
@@ -513,6 +593,7 @@
         dma = pltpu.SemaphoreType.DMA
         f32 = jnp.float32
         shapes = ((nf, levels, rows, lons), (levels, rows, lons), (nf, levels, half, lons))
+        held_bytes = sum(4 * math.prod(shape) for shape in shapes)
         held = pl.pallas_call(
             make_kernel(lat_count, lev_count, nf, levels, rows, lons),
             out_shape=tuple(pltpu.VMEM(shape, f32) for shape in shapes),
@@ -542,12 +623,14 @@
                 dma((2,)),
                 dma((lev_count - 1,)),
                 dma((lev_count - 1,)),
-                dma((nf, levels)),
-                dma((nf, levels)),
+                dma((nf - 1, levels, half // SUBS)),
+                dma((nf - 1, levels, half // SUBS)),
+                dma((levels,)),
+                dma((levels,)),
                 dma((2,)),
             ],
             compiler_params=pltpu.CompilerParams(
-                collective_id=0, has_side_effects=True, vmem_limit_bytes=40 * 1024 * 1024
+                collective_id=0, has_side_effects=True, vmem_limit_bytes=67043328 - held_bytes
             ),
             name="step",
         )(fields, velocity, surface, thickness, row_owner)
@@ -556,7 +639,7 @@
             out_shape=tuple(jax.ShapeDtypeStruct(shape, f32) for shape in shapes),
             in_specs=[pl.BlockSpec(memory_space=pl.ANY)] * 3,
             out_specs=[hbm_spec] * 3,
-            scratch_shapes=[dma((3,))],
+            scratch_shapes=[dma((levels * (2 * nf + 1),))],
             compiler_params=pltpu.CompilerParams(vmem_limit_bytes=1024 * 1024),
             name="write",
         )(*held)

time: 89 us -> 82.3 us (0.925)
  the two profiles are of different devices: /device:TPU:32 before, /device:TPU:38 now
where the time goes in v3:
time: 82.3 us; the launch traced here: 82.2 us
  Pallas kernels  81.5 us (99%)
    pallas_call x1, Pallas kernels, local(): pl.pallas_call(make_kernel(lat_count, lev_count, nf, levels, rows, lons),...  77.1 us
    pallas_call x1, Pallas kernels, local(): pl.pallas_call(write_out, out_shape=tuple((jax.ShapeDtypeStruct(shape, f3...  4.47 us

profile of v3, /device:TPU:38, one launch (start us, length us, event | category | flops | bytes accessed | tf_op | source)
XLA Modules:
  0.0 82.2 jit_solution(365423467105897148)
XLA Ops:
  0.6 77.1 %step.1 = (f32[3,4,32,4096]{3,2,1,0:T(8,128)S(1)}, f32[4,32,4096]{2,1,0:T(8,128)S(1)}, f32[3,4,16,4096]{3,2,1,0:T(8,128)S(1)}) custom-call(f32[3,4,32,4096]{3,2,1,0:T(8,128)} %fields.1, f32[2,4,32,4096]{3,2,1,0:T(8,128)} %velocity.1, f32[32,4096]{1,0:T(8,128)} %surface.1, f32[4]{0:T(128)} %thickness.1, s32[32]{0:T(128)} %row_owner.1), custom_call_target="tpu_custom_call" | custom-call | tf_op jit(solution)/shard_map/step/pallas_call | solution.py:597
  77.7 4.5 %write.1 = (f32[3,4,32,4096]{3,2,1,0:T(8,128)}, f32[4,32,4096]{2,1,0:T(8,128)}, f32[3,4,16,4096]{3,2,1,0:T(8,128)}) custom-call(f32[3,4,32,4096]{3,2,1,0:T(8,128)S(1)} %get-tuple-element.6.new_fields, f32[4,32,4096]{2,1,0:T(8,128)S(1)} %get-tuple-element.7.geo, f32[3,4,16,4096]{3,2,1,0:T(8,128)S(1)} %get-tuple-element.8.polar_rows), custom_call_target="tpu_custom_call" | custom-call | tf_op jit(solution)/shard_map/write/pallas_call | solution.py:637

commit v4 on v3

--- a/solution.py
+++ b/solution.py
@@ -52,8 +52,7 @@
         new_fields, geo, polar_rows,
         cells, wind, ground, halo, below, columns, packed, landed, front, back,
         tables, factor, factor_out, owners, thick, slots,
-        in_sem, wind_sem, small_sem, halo_send, halo_recv, col_send, col_recv, early_send,
-        early_recv, late_send, late_recv, factor_sem,
+        detour, in_sem, halo_sem, col_sem, send_sem, recv_sem, factor_sem, detour_sem,
     ):
         me = lax.axis_index("lat")
         lev = lax.axis_index("lev")
@@ -61,18 +60,23 @@
         plain = jnp.logical_not(polar)
         partner = lax.rem(me + shift, lat_count)
 
-        def cell_copy(q, k):
-            return pltpu.make_async_copy(fields.at[q, k], cells.at[q, k], in_sem.at[q, k])
-
-        def wind_copy(k, part):
-            return pltpu.make_async_copy(velocity.at[part, k], wind.at[part, k], wind_sem.at[part, k])
-
-        own_copy = pltpu.make_async_copy(row_owner, owners, small_sem.at[0])
-        thick_copy = pltpu.make_async_copy(thickness, thick, small_sem.at[1])
-        ground_copy = pltpu.make_async_copy(surface, ground, small_sem.at[2])
+        spans = (pl.ds(levels - 1, 1), pl.ds(levels - 2, 1), pl.ds(0, levels - 2))
+
+        def load(index):
+            span = spans[index]
+            return (
+                pltpu.make_async_copy(fields.at[0, span], cells.at[0, span], in_sem.at[2 * index]),
+                pltpu.make_async_copy(velocity.at[:, span], wind.at[:, span], in_sem.at[2 * index + 1]),
+            )
+
+        others = pl.ds(1, nf - 1)
+        load_others = pltpu.make_async_copy(fields.at[others], cells.at[others], in_sem.at[6])
+        own_copy = pltpu.make_async_copy(row_owner, owners, in_sem.at[7])
+        thick_copy = pltpu.make_async_copy(thickness, thick, in_sem.at[8])
+        ground_copy = pltpu.make_async_copy(surface, ground, in_sem.at[9])
 
         barrier = pltpu.get_barrier_semaphore()
-        for by in (shift, 1, lat_count - 1):
+        for by in (shift, 1, lat_count - 1, quarter, lat_count - quarter):
             pl.semaphore_signal(
                 barrier, inc=1, device_id={"lat": lax.rem(me + by, lat_count)}, device_id_type=MESH
             )
@@ -81,15 +85,12 @@
                 barrier, inc=1, device_id={"lev": lax.rem(lev + by, lev_count)}, device_id_type=MESH
             )
 
-        for q in range(nf):
-            for k in reversed(range(levels)):
-                cell_copy(q, k).start()
-                if q == 0:
-                    wind_copy(k, 0).start()
-                    wind_copy(k, 1).start()
-                    if k == levels - 1:
-                        own_copy.start()
-                        thick_copy.start()
+        own_copy.start()
+        for index in range(3):
+            for copy in load(index):
+                copy.start()
+        load_others.start()
+        thick_copy.start()
         ground_copy.start()
 
         row_ids = (me * rows + lax.broadcasted_iota(jnp.int32, (rows, LANES), 0)).astype(jnp.float32)
@@ -110,7 +111,6 @@
             front[at : at + SUBS, :] = jnp.zeros((SUBS, LANES), jnp.float32)
 
         own_copy.wait()
-        thick_copy.wait()
         sent, kept = [], []
         for row in range(rows):
             away = (owners[row] != me).astype(jnp.int32)
@@ -128,16 +128,16 @@
 
         north_copy = pltpu.make_async_remote_copy(
             src_ref=fields.at[:, :, rows - 1 : rows, :], dst_ref=halo.at[0],
-            send_sem=halo_send.at[0], recv_sem=halo_recv.at[0],
+            send_sem=halo_sem.at[0], recv_sem=halo_sem.at[1],
             device_id={"lat": lax.rem(me + 1, lat_count)}, device_id_type=MESH,
         )
         south_copy = pltpu.make_async_remote_copy(
             src_ref=fields.at[:, :, 0:1, :], dst_ref=halo.at[1],
-            send_sem=halo_send.at[1], recv_sem=halo_recv.at[1],
+            send_sem=halo_sem.at[0], recv_sem=halo_sem.at[1],
             device_id={"lat": lax.rem(me + lat_count - 1, lat_count)}, device_id_type=MESH,
         )
-        own_south = pltpu.make_async_copy(fields.at[:, :, 0:1, :], halo.at[0], halo_recv.at[0])
-        own_north = pltpu.make_async_copy(fields.at[:, :, rows - 1 : rows, :], halo.at[1], halo_recv.at[1])
+        own_south = pltpu.make_async_copy(fields.at[:, :, 0:1, :], halo.at[0], halo_sem.at[1])
+        own_north = pltpu.make_async_copy(fields.at[:, :, rows - 1 : rows, :], halo.at[1], halo_sem.at[1])
         first = me == 0
         last = me == lat_count - 1
 
@@ -146,26 +146,58 @@
             device_id={"lat": partner}, device_id_type=MESH,
         )
 
-        def early_copy(q, k, part):
-            span = pl.ds(part * SUBS, SUBS)
+        def row_copy(source, target, part, device=partner):
             return pltpu.make_async_remote_copy(
-                src_ref=packed.at[q, k, span], dst_ref=landed.at[q, k, span],
-                send_sem=early_send.at[q, k, part], recv_sem=early_recv.at[q, k, part],
-                device_id={"lat": partner}, device_id_type=MESH,
-            )
-
-        def late_copy(k):
+                src_ref=source, dst_ref=target, send_sem=send_sem.at[0], recv_sem=recv_sem.at[part],
+                device_id={"lat": device}, device_id_type=MESH,
+            )
+
+        def early_copy(*place):
+            return row_copy(packed.at[place], landed.at[place], place[0])
+
+        def field_copy(q):
+            return row_copy(packed.at[q], landed.at[q] if q < last_q else polar_rows.at[q], q)
+
+        onward = lax.rem(me + quarter, lat_count)
+        column = lax.rem(me, quarter) // 2
+        turn = (last_q - 1, levels - 1, pl.ds(half - SUBS, SUBS))
+
+        def detour_in(width):
             return pltpu.make_async_remote_copy(
-                src_ref=packed.at[last_q, k], dst_ref=polar_rows.at[last_q, k],
-                send_sem=late_send.at[k], recv_sem=late_recv.at[k],
-                device_id={"lat": partner}, device_id_type=MESH,
-            )
+                src_ref=packed.at[(*turn, pl.ds(0, width))], dst_ref=detour.at[:, pl.ds(0, width)],
+                send_sem=send_sem.at[0], recv_sem=detour_sem.at[0],
+                device_id={"lat": onward}, device_id_type=MESH,
+            )
+
+        def detour_out(width):
+            return pltpu.make_async_remote_copy(
+                src_ref=detour.at[:, pl.ds(0, width)], dst_ref=landed.at[(*turn, pl.ds(0, width))],
+                send_sem=detour_sem.at[1], recv_sem=recv_sem.at[last_q - 1],
+                device_id={"lat": onward}, device_id_type=MESH,
+            )
+
+        far = column == quarter // 2 - 1
+        detours = ((lons // 2, (column > 0) & jnp.logical_not(far)), (3 * lons // 4, far))
+        above = me >= lat_count - quarter
+        under = me < quarter
 
         def col_copy(by):
             return pltpu.make_async_remote_copy(
-                src_ref=below, dst_ref=columns.at[by - 1],
-                send_sem=col_send.at[by - 1], recv_sem=col_recv.at[by - 1],
+                src_ref=below, dst_ref=columns.at[by - 1], send_sem=col_sem.at[0], recv_sem=col_sem.at[1],
                 device_id={"lev": lax.rem(lev + lev_count - by, lev_count)}, device_id_type=MESH,
+            )
+
+        def col_copies(n):
+            return pltpu.make_async_remote_copy(
+                src_ref=columns.at[pl.ds(0, n)], dst_ref=columns.at[pl.ds(0, n)],
+                send_sem=col_sem.at[0], recv_sem=col_sem.at[1],
+                device_id={"lev": lax.rem(lev + 1, lev_count)}, device_id_type=MESH,
+            )
+
+        def halo_copies(ref):
+            return pltpu.make_async_remote_copy(
+                src_ref=ref, dst_ref=ref, send_sem=halo_sem.at[0], recv_sem=halo_sem.at[1],
+                device_id={"lat": partner}, device_id_type=MESH,
             )
 
         sub = lax.broadcasted_iota(jnp.int32, (SUBS, CHUNK), 0)
@@ -213,10 +245,10 @@
 
             lax.fori_loop(0, chunks, one, 0)
 
-        def pack(q, k, chosen, start=0):
+        def pack(q, k, chosen, start=0, cols=slice(None)):
             for place, slot in enumerate(chosen):
-                packed[q, k, start + place : start + place + 1, :] = new_fields[
-                    q, k, pl.ds(slots[slot], 1), :
+                packed[q, k, start + place : start + place + 1, cols] = new_fields[
+                    q, k, pl.ds(slots[slot], 1), cols
                 ]
 
         def keep(q, k):
@@ -224,21 +256,22 @@
                 polar_rows[q, k, slot : slot + 1, :] = new_fields[q, k, pl.ds(slots[half + slot], 1), :]
 
         def first_level(k):
-            cell_copy(0, k).wait()
-            wind_copy(k, 0).wait()
-            wind_copy(k, 1).wait()
             advect_level(0, k, False)
 
             @pl.when(polar)
             def _():
                 pack(0, k, order[:SUBS])
 
+        def send_first(k):
+            @pl.when(polar)
+            def _():
+                early_copy(0, k, pl.ds(0, SUBS)).start()
+
+        for copy in load(0):
+            copy.wait()
         first_level(levels - 1)
-        pl.semaphore_wait(barrier, 3 + lev_count - 1)
-
-        @pl.when(polar)
-        def _():
-            early_copy(0, levels - 1, 0).start()
+        pl.semaphore_wait(barrier, 5 + lev_count - 1)
+        send_first(levels - 1)
 
         @pl.when(jnp.logical_not(last))
         def _():
@@ -258,12 +291,14 @@
 
         def other_levels(index, carry):
             k = levels - 2 - index
+            for stage in range(1, 3):
+                @pl.when(index == stage - 1)
+                def _():
+                    for copy in load(stage):
+                        copy.wait()
+
             first_level(k)
-
-            @pl.when(polar)
-            def _():
-                early_copy(0, k, 0).start()
-
+            send_first(k)
             return carry
 
         lax.fori_loop(0, levels - 1, other_levels, 0)
@@ -282,21 +317,7 @@
         def _():
             factor_copy.start()
 
-        @pl.when(first)
-        def _():
-            own_south.wait()
-
-        @pl.when(jnp.logical_not(first))
-        def _():
-            north_copy.wait_recv()
-
-        @pl.when(last)
-        def _():
-            own_north.wait()
-
-        @pl.when(jnp.logical_not(last))
-        def _():
-            south_copy.wait_recv()
+        halo_copies(halo).wait_recv()
 
         def mend_edges(k, part):
             cols = pl.ds(pl.multiple_of(part * CHUNK, LANES), CHUNK)
@@ -325,11 +346,16 @@
             @pl.when(polar)
             def _():
                 pack(0, k, order[SUBS:], SUBS)
-                early_copy(0, k, 1).start()
 
             return carry
 
         lax.fori_loop(0, levels, mend_level, 0)
+
+        @pl.when(polar)
+        def _():
+            early_copy(0, slice(None), pl.ds(SUBS, half - SUBS)).start()
+
+        thick_copy.wait()
 
         def add_levels(index, carry):
             cols = pl.ds(pl.multiple_of(index * CHUNK, LANES), CHUNK)
@@ -352,21 +378,43 @@
 
         fill_slots(kept, half)
 
+        load_others.wait()
+
         def next_field(index, carry):
             q = 1 + index // levels
             k = levels - 1 - lax.rem(index, levels)
-            cell_copy(q, k).wait()
             advect_level(q, k, True)
 
             @pl.when(polar & (q < last_q))
             def _():
                 pack(q, k, order)
-                for part in range(half // SUBS):
-                    early_copy(q, k, part).start()
 
             return carry
 
-        lax.fori_loop(0, slabs - levels, next_field, 0)
+        lax.fori_loop(0, levels, next_field, 0)
+
+        for width, chosen in detours:
+            @pl.when(above & chosen)
+            def _():
+                detour_in(width).start()
+                early_copy(*turn, pl.ds(width, lons - width)).start()
+
+        @pl.when(polar & jnp.logical_not(above & (column > 0)))
+        def _():
+            early_copy(*turn, slice(None)).start()
+
+        @pl.when(polar)
+        def _():
+            early_copy(last_q - 1, levels - 1, pl.ds(0, half - SUBS)).start()
+            early_copy(last_q - 1, pl.ds(0, levels - 1)).start()
+
+        lax.fori_loop(levels, slabs - levels, next_field, 0)
+
+        for width, chosen in detours:
+            @pl.when(under & chosen)
+            def _():
+                detour_in(width).wait_recv()
+                detour_out(width).start()
 
         def place_of(block):
             return lax.rem(block, per_segment) * LANES + PAD, block // per_segment
@@ -456,12 +504,10 @@
 
             @pl.when(plain & (index < last_q))
             def _():
-                def heard(k, carry):
-                    for part in range(half // SUBS):
-                        early_copy(index, levels - 1 - k, part).wait_recv()
-                    return carry
-
-                lax.fori_loop(0, levels, heard, 0)
+                for q in range(last_q):
+                    @pl.when(index == q)
+                    def _():
+                        field_copy(q).wait_recv()
 
                 def fill(place, carry):
                     for block in (place * UNROLL + i for i in range(UNROLL)):
@@ -490,10 +536,10 @@
                 def _():
                     def send(k, carry):
                         pack(last_q, k, range(half))
-                        late_copy(k).start()
                         return carry
 
                     lax.fori_loop(0, levels, send, 0)
+                    field_copy(last_q).start()
 
                 def hold(k, carry):
                     keep(q, k)
@@ -519,10 +565,10 @@
         lax.fori_loop(0, nf, job, 0)
 
         ground_copy.wait()
-        for by in range(1, lev_count):
-            @pl.when(lev + by < lev_count)
-            def _():
-                col_copy(by).wait_recv()
+        for n in range(1, lev_count):
+            @pl.when(lev == lev_count - 1 - n)
+            def _():
+                col_copies(n).wait_recv()
 
         def finish(index, carry):
             span = pl.ds(pl.multiple_of(index * SUBS, SUBS), SUBS)
@@ -535,46 +581,42 @@
 
         lax.fori_loop(0, groups, finish, 0)
 
-        for by in range(1, lev_count):
-            @pl.when(lev >= by)
-            def _():
-                col_copy(by).wait_send()
-
-        @pl.when(jnp.logical_not(last))
-        def _():
-            north_copy.wait_send()
-
-        @pl.when(jnp.logical_not(first))
-        def _():
-            south_copy.wait_send()
+        for n in range(1, lev_count):
+            @pl.when(lev == n)
+            def _():
+                col_copies(n).wait_send()
+
+        @pl.when(first | last)
+        def _():
+            halo_copies(halo.at[0]).wait_send()
+
+        @pl.when(jnp.logical_not(first | last))
+        def _():
+            halo_copies(halo).wait_send()
+
+        for width, chosen in detours:
+            @pl.when(under & chosen)
+            def _():
+                detour_out(width).wait_send()
 
         @pl.when(polar)
         def _():
             factor_copy.wait_send()
-            for q in range(last_q):
-                for k in range(levels):
-                    for part in range(half // SUBS):
-                        early_copy(q, k, part).wait_send()
-            for k in range(levels):
-                late_copy(k).wait_send()
+            row_copy(packed, polar_rows, last_q).wait_send()
 
         @pl.when(plain)
         def _():
-            for k in range(levels):
-                late_copy(k).wait_recv()
+            field_copy(last_q).wait_recv()
 
     return kernel
 
 
 def write_out(new_fields, geo, polar_rows, new_fields_out, geo_out, polar_rows_out, sem):
-    levels = geo.shape[0]
-    copies = []
-    for k in range(levels):
-        for q in range(new_fields.shape[0]):
-            copies.append((new_fields.at[q, k], new_fields_out.at[q, k]))
-            copies.append((polar_rows.at[q, k], polar_rows_out.at[q, k]))
-        copies.append((geo.at[k], geo_out.at[k]))
-    copies = [pltpu.make_async_copy(*pair, sem.at[i]) for i, pair in enumerate(copies)]
+    copies = [
+        pltpu.make_async_copy(new_fields, new_fields_out, sem.at[0]),
+        pltpu.make_async_copy(geo, geo_out, sem.at[1]),
+        pltpu.make_async_copy(polar_rows, polar_rows_out, sem.at[2]),
+    ]
     for copy in copies:
         copy.start()
     for copy in copies:
@@ -616,17 +658,13 @@
                 pltpu.SMEM((rows,), jnp.int32),
                 pltpu.SMEM((levels,), f32),
                 pltpu.SMEM((rows,), jnp.int32),
-                dma((nf, levels)),
-                dma((2, levels)),
-                dma((3,)),
+                pltpu.VMEM((SUBS, 3 * lons // 4), f32),
+                dma((10,)),
                 dma((2,)),
                 dma((2,)),
-                dma((lev_count - 1,)),
-                dma((lev_count - 1,)),
-                dma((nf - 1, levels, half // SUBS)),
-                dma((nf - 1, levels, half // SUBS)),
-                dma((levels,)),
-                dma((levels,)),
+                dma((1,)),
+                dma((nf,)),
+                dma((2,)),
                 dma((2,)),
             ],
             compiler_params=pltpu.CompilerParams(
@@ -639,7 +677,7 @@
             out_shape=tuple(jax.ShapeDtypeStruct(shape, f32) for shape in shapes),
             in_specs=[pl.BlockSpec(memory_space=pl.ANY)] * 3,
             out_specs=[hbm_spec] * 3,
-            scratch_shapes=[dma((levels * (2 * nf + 1),))],
+            scratch_shapes=[dma((3,))],
             compiler_params=pltpu.CompilerParams(vmem_limit_bytes=1024 * 1024),
             name="write",
         )(*held)

time: 82.3 us -> 79.6 us (0.967)
  Pallas kernels: 81.5 us -> 78.8 us
    pallas_call x1, Pallas kernels: 77.1 us -> 74.5 us  [local(): pl.pallas_call(make_kernel(lat_count, lev_count, nf, levels, rows, lons),...]
where the time goes in v4:
time: 79.6 us; the launch traced here: 79.5 us
  Pallas kernels  78.8 us (99%)
    pallas_call x1, Pallas kernels, local(): pl.pallas_call(make_kernel(lat_count, lev_count, nf, levels, rows, lons),...  74.5 us
    pallas_call x1, Pallas kernels, local(): pl.pallas_call(write_out, out_shape=tuple((jax.ShapeDtypeStruct(shape, f3...  4.39 us

profile of v4, /device:TPU:38, one launch (start us, length us, event | category | flops | bytes accessed | tf_op | source)
XLA Modules:
  0.0 79.5 jit_solution(9765313860711046088)
XLA Ops:
  0.6 74.5 %step.1 = (f32[3,4,32,4096]{3,2,1,0:T(8,128)S(1)}, f32[4,32,4096]{2,1,0:T(8,128)S(1)}, f32[3,4,16,4096]{3,2,1,0:T(8,128)S(1)}) custom-call(f32[3,4,32,4096]{3,2,1,0:T(8,128)} %fields.1, f32[2,4,32,4096]{3,2,1,0:T(8,128)} %velocity.1, f32[32,4096]{1,0:T(8,128)} %surface.1, f32[4]{0:T(128)} %thickness.1, s32[32]{0:T(128)} %row_owner.1), custom_call_target="tpu_custom_call" | custom-call | tf_op jit(solution)/shard_map/step/pallas_call | solution.py:639
  75.1 4.4 %write.1 = (f32[3,4,32,4096]{3,2,1,0:T(8,128)}, f32[4,32,4096]{2,1,0:T(8,128)}, f32[3,4,16,4096]{3,2,1,0:T(8,128)}) custom-call(f32[3,4,32,4096]{3,2,1,0:T(8,128)S(1)} %get-tuple-element.6.new_fields, f32[4,32,4096]{2,1,0:T(8,128)S(1)} %get-tuple-element.7.geo, f32[3,4,16,4096]{3,2,1,0:T(8,128)S(1)} %get-tuple-element.8.polar_rows), custom_call_target="tpu_custom_call" | custom-call | tf_op jit(solution)/shard_map/write/pallas_call | solution.py:675

commit v5 on v4

--- a/solution.py
+++ b/solution.py
@@ -52,7 +52,7 @@
         new_fields, geo, polar_rows,
         cells, wind, ground, halo, below, columns, packed, landed, front, back,
         tables, factor, factor_out, owners, thick, slots,
-        detour, in_sem, halo_sem, col_sem, send_sem, recv_sem, factor_sem, detour_sem,
+        detour, passing, pass_sem, in_sem, halo_sem, col_sem, send_sem, recv_sem, factor_sem, detour_sem,
     ):
         me = lax.axis_index("lat")
         lev = lax.axis_index("lev")
@@ -76,10 +76,42 @@
         ground_copy = pltpu.make_async_copy(surface, ground, in_sem.at[9])
 
         barrier = pltpu.get_barrier_semaphore()
-        for by in (shift, 1, lat_count - 1, quarter, lat_count - quarter):
+        first = me == 0
+        last = me == lat_count - 1
+        for by in (shift, quarter, lat_count - quarter):
             pl.semaphore_signal(
                 barrier, inc=1, device_id={"lat": lax.rem(me + by, lat_count)}, device_id_type=MESH
             )
+
+        @pl.when(jnp.logical_not(last))
+        def _():
+            pl.semaphore_signal(barrier, inc=1, device_id={"lat": me + 1}, device_id_type=MESH)
+
+        @pl.when(jnp.logical_not(first))
+        def _():
+            pl.semaphore_signal(barrier, inc=1, device_id={"lat": me - 1}, device_id_type=MESH)
+
+        middle = 2 * quarter
+        routes = (
+            (0, quarter - 1, quarter + 4, levels // 2),
+            (1, lat_count - quarter, middle + 2, levels // 2),
+            (0, middle - 1, middle + 4, levels // 2),
+            (1, middle, quarter + 2, levels // 2),
+        )
+        greetings = {}
+        for side, sender, via, _ in routes:
+            target = sender + (1, -1)[side]
+            for one, other in ((sender, via), (via, target)):
+                greetings.setdefault(one, []).append(other)
+                greetings.setdefault(other, []).append(one)
+        for here, friends in greetings.items():
+            @pl.when(me == here)
+            def _():
+                for there in friends:
+                    pl.semaphore_signal(
+                        barrier, inc=1, device_id={"lat": there}, device_id_type=MESH
+                    )
+
         for by in range(1, lev_count):
             pl.semaphore_signal(
                 barrier, inc=1, device_id={"lev": lax.rem(lev + by, lev_count)}, device_id_type=MESH
@@ -126,20 +158,32 @@
 
         fill_slots(sent, 0)
 
-        north_copy = pltpu.make_async_remote_copy(
-            src_ref=fields.at[:, :, rows - 1 : rows, :], dst_ref=halo.at[0],
-            send_sem=halo_sem.at[0], recv_sem=halo_sem.at[1],
-            device_id={"lat": lax.rem(me + 1, lat_count)}, device_id_type=MESH,
-        )
-        south_copy = pltpu.make_async_remote_copy(
-            src_ref=fields.at[:, :, 0:1, :], dst_ref=halo.at[1],
-            send_sem=halo_sem.at[0], recv_sem=halo_sem.at[1],
-            device_id={"lat": lax.rem(me + lat_count - 1, lat_count)}, device_id_type=MESH,
-        )
+        every = pl.ds(0, levels)
+        edge = (pl.ds(rows - 1, 1), pl.ds(0, 1))
+
+        def halo_copy(side, span):
+            return pltpu.make_async_remote_copy(
+                src_ref=fields.at[:, span, edge[side], :], dst_ref=halo.at[side, :, span],
+                send_sem=halo_sem.at[0], recv_sem=halo_sem.at[1],
+                device_id={"lat": lax.rem(me + (1, lat_count - 1)[side], lat_count)}, device_id_type=MESH,
+            )
+
+        def pass_in(side, sender, via, count):
+            return pltpu.make_async_remote_copy(
+                src_ref=fields.at[:, pl.ds(0, count), edge[side], :], dst_ref=passing.at[:, pl.ds(0, count)],
+                send_sem=halo_sem.at[0], recv_sem=pass_sem.at[0],
+                device_id={"lat": via}, device_id_type=MESH,
+            )
+
+        def pass_out(side, sender, via, count):
+            return pltpu.make_async_remote_copy(
+                src_ref=passing.at[:, pl.ds(0, count)], dst_ref=halo.at[side, :, pl.ds(0, count)],
+                send_sem=pass_sem.at[1], recv_sem=halo_sem.at[1],
+                device_id={"lat": sender + (1, -1)[side]}, device_id_type=MESH,
+            )
+
         own_south = pltpu.make_async_copy(fields.at[:, :, 0:1, :], halo.at[0], halo_sem.at[1])
         own_north = pltpu.make_async_copy(fields.at[:, :, rows - 1 : rows, :], halo.at[1], halo_sem.at[1])
-        first = me == 0
-        last = me == lat_count - 1
 
         factor_copy = pltpu.make_async_remote_copy(
             src_ref=factor_out, dst_ref=factor, send_sem=factor_sem.at[0], recv_sem=factor_sem.at[1],
@@ -176,8 +220,8 @@
                 device_id={"lat": onward}, device_id_type=MESH,
             )
 
-        far = column == quarter // 2 - 1
-        detours = ((lons // 2, (column > 0) & jnp.logical_not(far)), (3 * lons // 4, far))
+        odd = lax.rem(column, 2) == 1
+        detours = ((lons // 4, jnp.logical_not(odd)), (5 * lons // 8, odd))
         above = me >= lat_count - quarter
         under = me < quarter
 
@@ -270,16 +314,28 @@
         for copy in load(0):
             copy.wait()
         first_level(levels - 1)
-        pl.semaphore_wait(barrier, 5 + lev_count - 1)
+
+        heard = 5 + lev_count - 1 - (first | last).astype(jnp.int32)
+        for here, friends in greetings.items():
+            heard = heard + (me == here).astype(jnp.int32) * len(friends)
+        pl.semaphore_wait(barrier, heard)
         send_first(levels - 1)
 
-        @pl.when(jnp.logical_not(last))
-        def _():
-            north_copy.start()
-
-        @pl.when(jnp.logical_not(first))
-        def _():
-            south_copy.start()
+        for side, end in ((0, last), (1, first)):
+            whole = jnp.logical_not(end)
+            for route in routes:
+                if route[0] == side:
+                    whole = whole & (me != route[1])
+
+            @pl.when(whole)
+            def _():
+                halo_copy(side, every).start()
+
+        for route in routes:
+            @pl.when(me == route[1])
+            def _():
+                pass_in(*route).start()
+                halo_copy(route[0], pl.ds(route[3], levels - route[3])).start()
 
         @pl.when(first)
         def _():
@@ -316,6 +372,12 @@
         @pl.when(polar)
         def _():
             factor_copy.start()
+
+        for route in routes:
+            @pl.when(me == route[2])
+            def _():
+                pass_in(*route).wait_recv()
+                pass_out(*route).start()
 
         halo_copies(halo).wait_recv()
 
@@ -399,7 +461,7 @@
                 detour_in(width).start()
                 early_copy(*turn, pl.ds(width, lons - width)).start()
 
-        @pl.when(polar & jnp.logical_not(above & (column > 0)))
+        @pl.when(polar & jnp.logical_not(above))
         def _():
             early_copy(*turn, slice(None)).start()
 
@@ -593,6 +655,11 @@
         @pl.when(jnp.logical_not(first | last))
         def _():
             halo_copies(halo).wait_send()
+
+        for route in routes:
+            @pl.when(me == route[2])
+            def _():
+                pass_out(*route).wait_send()
 
         for width, chosen in detours:
             @pl.when(under & chosen)
@@ -658,7 +725,9 @@
                 pltpu.SMEM((rows,), jnp.int32),
                 pltpu.SMEM((levels,), f32),
                 pltpu.SMEM((rows,), jnp.int32),
-                pltpu.VMEM((SUBS, 3 * lons // 4), f32),
+                pltpu.VMEM((SUBS, 5 * lons // 8), f32),
+                pltpu.VMEM((nf, levels // 2, 1, lons), f32),
+                dma((2,)),
                 dma((10,)),
                 dma((2,)),
                 dma((2,)),

time: 79.6 us -> 78.9 us (level)
  no operation moved by 1% of the time
where the time goes in v5:
time: 78.9 us; the launch traced here: 78.8 us
  Pallas kernels  78.2 us (99%)
    pallas_call x1, Pallas kernels, local(): pl.pallas_call(make_kernel(lat_count, lev_count, nf, levels, rows, lons),...  73.8 us
    pallas_call x1, Pallas kernels, local(): pl.pallas_call(write_out, out_shape=tuple((jax.ShapeDtypeStruct(shape, f3...  4.39 us

profile of v5, /device:TPU:38, one launch (start us, length us, event | category | flops | bytes accessed | tf_op | source)
XLA Modules:
  0.0 78.8 jit_solution(5312332653599522589)
XLA Ops:
  0.6 73.8 %step.1 = (f32[3,4,32,4096]{3,2,1,0:T(8,128)S(1)}, f32[4,32,4096]{2,1,0:T(8,128)S(1)}, f32[3,4,16,4096]{3,2,1,0:T(8,128)S(1)}) custom-call(f32[3,4,32,4096]{3,2,1,0:T(8,128)} %fields.1, f32[2,4,32,4096]{3,2,1,0:T(8,128)} %velocity.1, f32[32,4096]{1,0:T(8,128)} %surface.1, f32[4]{0:T(128)} %thickness.1, s32[32]{0:T(128)} %row_owner.1), custom_call_target="tpu_custom_call" | custom-call | tf_op jit(solution)/shard_map/step/pallas_call | solution.py:706
  74.4 4.4 %write.1 = (f32[3,4,32,4096]{3,2,1,0:T(8,128)}, f32[4,32,4096]{2,1,0:T(8,128)}, f32[3,4,16,4096]{3,2,1,0:T(8,128)}) custom-call(f32[3,4,32,4096]{3,2,1,0:T(8,128)S(1)} %get-tuple-element.6.new_fields, f32[4,32,4096]{2,1,0:T(8,128)S(1)} %get-tuple-element.7.geo, f32[3,4,16,4096]{3,2,1,0:T(8,128)S(1)} %get-tuple-element.8.polar_rows), custom_call_target="tpu_custom_call" | custom-call | tf_op jit(solution)/shard_map/write/pallas_call | solution.py:744

commit v6 on v5

--- a/solution.py
+++ b/solution.py
@@ -78,18 +78,33 @@
         barrier = pltpu.get_barrier_semaphore()
         first = me == 0
         last = me == lat_count - 1
+
+        @pl.when(jnp.logical_not(last))
+        def _():
+            pl.semaphore_signal(barrier, inc=1, device_id={"lat": me + 1}, device_id_type=MESH)
+
+        @pl.when(jnp.logical_not(first))
+        def _():
+            pl.semaphore_signal(barrier, inc=1, device_id={"lat": me - 1}, device_id_type=MESH)
+
+
+        for by in range(1, lev_count):
+            pl.semaphore_signal(
+                barrier, inc=1, device_id={"lev": lax.rem(lev + by, lev_count)}, device_id_type=MESH
+            )
+
         for by in (shift, quarter, lat_count - quarter):
             pl.semaphore_signal(
                 barrier, inc=1, device_id={"lat": lax.rem(me + by, lat_count)}, device_id_type=MESH
             )
 
-        @pl.when(jnp.logical_not(last))
-        def _():
-            pl.semaphore_signal(barrier, inc=1, device_id={"lat": me + 1}, device_id_type=MESH)
-
-        @pl.when(jnp.logical_not(first))
-        def _():
-            pl.semaphore_signal(barrier, inc=1, device_id={"lat": me - 1}, device_id_type=MESH)
+        own_copy.start()
+        for index in range(3):
+            for copy in load(index):
+                copy.start()
+        load_others.start()
+        thick_copy.start()
+        ground_copy.start()
 
         middle = 2 * quarter
         routes = (
@@ -111,19 +126,6 @@
                     pl.semaphore_signal(
                         barrier, inc=1, device_id={"lat": there}, device_id_type=MESH
                     )
-
-        for by in range(1, lev_count):
-            pl.semaphore_signal(
-                barrier, inc=1, device_id={"lev": lax.rem(lev + by, lev_count)}, device_id_type=MESH
-            )
-
-        own_copy.start()
-        for index in range(3):
-            for copy in load(index):
-                copy.start()
-        load_others.start()
-        thick_copy.start()
-        ground_copy.start()
 
         row_ids = (me * rows + lax.broadcasted_iota(jnp.int32, (rows, LANES), 0)).astype(jnp.float32)
         lat_mid = -0.5 * math.pi + (row_ids + 0.5) * spacing

time: 78.9 us -> 78.9 us (level)
  no operation moved by 1% of the time
where the time goes in v6:
time: 78.9 us; the launch traced here: 78.8 us
  Pallas kernels  78.1 us (99%)
    pallas_call x1, Pallas kernels, local(): pl.pallas_call(make_kernel(lat_count, lev_count, nf, levels, rows, lons),...  73.7 us
    pallas_call x1, Pallas kernels, local(): pl.pallas_call(write_out, out_shape=tuple((jax.ShapeDtypeStruct(shape, f3...  4.39 us

profile of v6, /device:TPU:38, one launch (start us, length us, event | category | flops | bytes accessed | tf_op | source)
XLA Modules:
  0.0 78.8 jit_solution(4670316267596819849)
XLA Ops:
  0.6 73.7 %step.1 = (f32[3,4,32,4096]{3,2,1,0:T(8,128)S(1)}, f32[4,32,4096]{2,1,0:T(8,128)S(1)}, f32[3,4,16,4096]{3,2,1,0:T(8,128)S(1)}) custom-call(f32[3,4,32,4096]{3,2,1,0:T(8,128)} %fields.1, f32[2,4,32,4096]{3,2,1,0:T(8,128)} %velocity.1, f32[32,4096]{1,0:T(8,128)} %surface.1, f32[4]{0:T(128)} %thickness.1, s32[32]{0:T(128)} %row_owner.1), custom_call_target="tpu_custom_call" | custom-call | tf_op jit(solution)/shard_map/step/pallas_call | solution.py:708
  74.4 4.4 %write.1 = (f32[3,4,32,4096]{3,2,1,0:T(8,128)}, f32[4,32,4096]{2,1,0:T(8,128)}, f32[3,4,16,4096]{3,2,1,0:T(8,128)}) custom-call(f32[3,4,32,4096]{3,2,1,0:T(8,128)S(1)} %get-tuple-element.6.new_fields, f32[4,32,4096]{2,1,0:T(8,128)S(1)} %get-tuple-element.7.geo, f32[3,4,16,4096]{3,2,1,0:T(8,128)S(1)} %get-tuple-element.8.polar_rows), custom_call_target="tpu_custom_call" | custom-call | tf_op jit(solution)/shard_map/write/pallas_call | solution.py:746
